TPU v7x, 256 devices: a whole 4x4x8 slice. The times are simulated.
256 devices in a mesh: seq: 128 (over z, y, x), head: 2 (over core).
Axes of the slice: x: 4, y: 4, z: 8, core: 2. Of those that a mesh axis runs over, the one named last changes fastest.
Arguments:
- queries: bfloat16 [65536, 2048], P(('seq', 'head')), may hold values from -6 to 6
- key_rows: bfloat16 [65536, 2048], P(('seq', 'head')), may hold values from -6 to 6
- values: bfloat16 [65536, 2048], P(('seq', 'head')), may hold values from -6 to 6
- out_grad: bfloat16 [65536, 2048], P(('seq', 'head')), may hold values from -6 to 6
- level_weights: float32 [16, 11], replicated, may hold values from 0.2 to 1
Outputs:
- query_grad: bfloat16 [65536, 2048], P(('seq', 'head'))
- key_grad: bfloat16 [65536, 2048], P(('seq', 'head'))
- value_grad: bfloat16 [65536, 2048], P(('seq', 'head'))
All inputs are finite; a program needn't handle non-finite values.
Results may differ from a plain program's by a relative error of at most 0.003.
Values may be sent and summed in bfloat16 or wider, within the bound.
A program may use at most 128 MiB of HBM per device.

v0:
```python
import jax
import jax.numpy as jnp
from jax import lax
from jax.sharding import PartitionSpec as P

DH = 128
BLOCK = 128


def partner(array, axis, distance):
    return lax.ppermute(array, axis, [(i, i ^ 1 << distance) for i in range(lax.axis_size(axis))])


def fenwick_local(kv_blocks, qo_blocks, level_scale):
    block_count = kv_blocks.shape[0]
    inner_shape = kv_blocks.shape[1:]
    earlier = jnp.zeros_like(kv_blocks)
    later = jnp.zeros_like(qo_blocks)
    for level_index in range(1, block_count.bit_length()):
        half_span = 1 << level_index - 1
        group_count = block_count >> level_index
        weight = level_scale[:, level_index][:, None, None]
        kv_groups = kv_blocks.reshape((group_count, 2, half_span) + inner_shape)
        qo_groups = qo_blocks.reshape((group_count, 2, half_span) + inner_shape)
        lower_sum = jnp.sum(kv_groups[:, 0], axis=1) * weight
        upper_sum = jnp.sum(qo_groups[:, 1], axis=1) * weight
        zero_block = jnp.zeros_like(lower_sum)
        add_earlier = jnp.stack([zero_block, lower_sum], axis=1)[:, :, None]
        add_later = jnp.stack([upper_sum, zero_block], axis=1)[:, :, None]
        full_shape = (group_count, 2, half_span) + inner_shape
        earlier = earlier + jnp.broadcast_to(add_earlier, full_shape).reshape(kv_blocks.shape)
        later = later + jnp.broadcast_to(add_later, full_shape).reshape(qo_blocks.shape)
    return (earlier, later)


def cross_states(kv_total, qo_total, level_scale, local_levels, swapper, position, chain_len):
    earlier = jnp.zeros_like(kv_total)
    later = jnp.zeros_like(qo_total)
    group_kv = kv_total
    group_qo = qo_total
    for bit_index in range(chain_len.bit_length() - 1):
        other_kv, other_qo = swapper((group_kv, group_qo), bit_index)
        upper_half = (position // (1 << bit_index) % 2).astype(jnp.float32)
        weight = level_scale[:, local_levels + 1 + bit_index][:, None, None]
        earlier = earlier + upper_half * weight * other_kv
        later = later + (1.0 - upper_half) * weight * other_qo
        group_kv = group_kv + other_kv
        group_qo = group_qo + other_qo
    return (earlier, later)


def range_grads(
    query_rows, key_part, value_rows, grad_rows, level_scale, swapper, position, chain_len
):
    high = lax.Precision.HIGHEST
    token_count = query_rows.shape[0]
    head_count = query_rows.shape[1] // DH
    block_count = token_count // BLOCK
    shape_four = (block_count, BLOCK, head_count, DH)
    query_blk = query_rows.reshape(shape_four)
    key_blk = key_part.reshape(shape_four)
    value_blk = value_rows.reshape(shape_four)
    grad_blk = grad_rows.reshape(shape_four)
    rows = lax.broadcasted_iota(jnp.int32, (BLOCK, BLOCK), 0)
    cols = lax.broadcasted_iota(jnp.int32, (BLOCK, BLOCK), 1)
    causal_mask = (rows >= cols).astype(jnp.float32)
    first_weight = level_scale[:, 0][None, :, None, None]
    kv_blocks = jnp.einsum(
        "nshd,nshe->nhde", key_blk, value_blk, preferred_element_type=jnp.float32
    )
    qo_blocks = jnp.einsum(
        "nthd,nthe->nhde", query_blk, grad_blk, preferred_element_type=jnp.float32
    )
    local_levels = block_count.bit_length() - 1
    earlier_dev, later_dev = cross_states(
        jnp.sum(kv_blocks, axis=0),
        jnp.sum(qo_blocks, axis=0),
        level_scale,
        local_levels,
        swapper,
        position,
        chain_len,
    )
    scores = jnp.einsum("nthd,nshd->nhts", query_blk, key_blk, preferred_element_type=jnp.float32)
    weighted = (scores * causal_mask * first_weight).astype(jnp.bfloat16)
    grad_prob = jnp.einsum(
        "nthe,nshe->nhts", grad_blk, value_blk, preferred_element_type=jnp.float32
    )
    grad_score = (grad_prob * causal_mask * first_weight).astype(jnp.bfloat16)
    value_local = jnp.einsum(
        "nhts,nthe->nshe", weighted, grad_blk, preferred_element_type=jnp.float32
    )
    query_local = jnp.einsum(
        "nhts,nshd->nthd", grad_score, key_blk, preferred_element_type=jnp.float32
    )
    key_local = jnp.einsum(
        "nhts,nthd->nshd", grad_score, query_blk, preferred_element_type=jnp.float32
    )
    earlier_local, later_local = fenwick_local(kv_blocks, qo_blocks, level_scale)
    earlier = earlier_local + earlier_dev[None]
    later = later_local + later_dev[None]
    query_cross = jnp.einsum(
        "nthe,nhde->nthd", grad_blk, earlier, precision=high, preferred_element_type=jnp.float32
    )
    key_cross = jnp.einsum(
        "nshe,nhde->nshd", value_blk, later, precision=high, preferred_element_type=jnp.float32
    )
    value_cross = jnp.einsum(
        "nshd,nhde->nshe", key_blk, later, precision=high, preferred_element_type=jnp.float32
    )
    flat_shape = (token_count, head_count * DH)
    return (
        (query_local + query_cross).astype(jnp.bfloat16).reshape(flat_shape),
        (key_local + key_cross).astype(jnp.bfloat16).reshape(flat_shape),
        (value_local + value_cross).astype(jnp.bfloat16).reshape(flat_shape),
    )


def body(queries, key_rows, values, out_grad, level_weights):
    level_ids = jnp.arange(level_weights.shape[1], dtype=jnp.float32)
    level_scale = (
        level_weights
        * jnp.exp2((1.0 - level_ids) / 2.0)[None, :]
        / jnp.sqrt(jnp.float32(DH * BLOCK))
    )
    query_rows, key_part, value_rows, grad_rows = (
        lax.all_to_all(queries, "head", split_axis=1, concat_axis=0, tiled=True),
        lax.all_to_all(key_rows, "head", split_axis=1, concat_axis=0, tiled=True),
        lax.all_to_all(values, "head", split_axis=1, concat_axis=0, tiled=True),
        lax.all_to_all(out_grad, "head", split_axis=1, concat_axis=0, tiled=True),
    )
    head_count = level_scale.shape[0] // lax.axis_size("head")
    head_scale = lax.dynamic_slice_in_dim(
        level_scale, lax.axis_index("head") * head_count, head_count, 0
    )

    def swap_heads(states, bit_index):
        return partner(states, "seq", bit_index)

    query_part, key_grad_part, value_part = range_grads(
        query_rows,
        key_part,
        value_rows,
        grad_rows,
        head_scale,
        swap_heads,
        lax.axis_index("seq"),
        lax.axis_size("seq"),
    )
    return (
        lax.all_to_all(query_part, "head", split_axis=0, concat_axis=1, tiled=True),
        lax.all_to_all(key_grad_part, "head", split_axis=0, concat_axis=1, tiled=True),
        lax.all_to_all(value_part, "head", split_axis=0, concat_axis=1, tiled=True),
    )


def solution(mesh):
    return jax.shard_map(
        body,
        mesh=mesh,
        in_specs=(
            P(("seq", "head"), None),
            P(("seq", "head"), None),
            P(("seq", "head"), None),
            P(("seq", "head"), None),
            P(),
        ),
        out_specs=(P(("seq", "head"), None), P(("seq", "head"), None), P(("seq", "head"), None)),
        check_vma=False,
    )
```

profile of v0, /device:TPU:1, one launch (start us, length us, event | category | flops | bytes accessed | tf_op | source)
XLA Modules:
  0.0 267.1 jit_solution(1590416939446828161)
XLA Ops:
  0.6 2.4 copy.180
  3.0 6.8 %all-to-all-start = ((bf16[256,2,1024]{2,0,1:T(8,128)(2,1)}), bf16[256,2,1024]{2,0,1:T(8,128)(2,1)S(1)}, u32[]{:S(2)}, u32[]{:S(2)}) async-start(bf16[256,2,1024]{2,0,1:T(8,128)(2,1)} %bitcast.96), calls=%async_computation | async-start | bytes 2097152 | tf_op jit(solution)/shard_map/all_to_all | solution.py:130
  11.6 3.9 %all-to-all-start.4 = ((bf16[256,2,1024]{2,0,1:T(8,128)(2,1)}), bf16[256,2,1024]{2,0,1:T(8,128)(2,1)S(1)}, u32[]{:S(2)}, u32[]{:S(2)}) async-start(bf16[256,2,1024]{2,0,1:T(8,128)(2,1)} %bitcast.93), calls=%async_computation.4 | async-start | bytes 2097152 | tf_op jit(solution)/shard_map/all_to_all | solution.py:127
  17.5 2.7 %fusion.31 = (f32[8,128,128]{2,1,0:T(8,128)}, f32[4,8,128,128]{3,2,1,0:T(8,128)}) fusion(bf16[4,128,8,128]{3,2,1,0:T(8,128)(2,1)S(1)} %bitcast.101, bf16[4,128,8,128]{3,2,1,0:T(8,128)(2,1)S(1)} %bitcast.105), kind=kOutput, calls=%fused_computation.72 | convolution fusion | flops 134610944 | bytes 4718592 | tf_op jit(solution)/shard_map/nthd,nthe->nhde/dot_general | solution.py:71
  21.3 3.9 %all-to-all-start.2 = ((bf16[256,2,1024]{2,0,1:T(8,128)(2,1)}), bf16[256,2,1024]{2,0,1:T(8,128)(2,1)S(1)}, u32[]{:S(2)}, u32[]{:S(2)}) async-start(bf16[256,2,1024]{2,0,1:T(8,128)(2,1)} %bitcast.119), calls=%async_computation.2 | async-start | bytes 2097152 | tf_op jit(solution)/shard_map/all_to_all | solution.py:128
  25.2 2.3 copy.179
  27.5 4.4 %all-to-all-start.1 = ((bf16[256,2,1024]{2,0,1:T(8,128)(2,1)}), bf16[256,2,1024]{2,0,1:T(8,128)(2,1)}, u32[]{:S(2)}, u32[]{:S(2)}) async-start(bf16[256,2,1024]{2,0,1:T(8,128)(2,1)} %bitcast.118), calls=%async_computation.1 | async-start | bytes 2097152 | tf_op jit(solution)/shard_map/all_to_all | solution.py:129
  32.0 1.5 copy.133
  33.8 1.5 copy.132
  35.3 2.6 fusion.30
  38.0 1.7 collective-permute-start
  39.7 2.0 add.176
  42.8 1.5 slice_reduce_fusion
  44.3 7.7 %collective-permute-done = f32[8,128,128]{2,1,0:T(8,128)} collective-permute-done((f32[8,128,128]{2,1,0:T(8,128)}, f32[8,128,128]{2,1,0:T(8,128)}, u32[]{:S(2)}, u32[]{:S(2)}) %collective-permute-start) | collective-permute-done | bytes 524320 | tf_op jit(solution)/shard_map/ppermute | solution.py:11
  53.3 1.7 collective-permute-start.1
  55.0 9.0 %collective-permute-done.8 = f32[8,128,128]{2,1,0:T(8,128)} collective-permute-done((f32[8,128,128]{2,1,0:T(8,128)}, f32[8,128,128]{2,1,0:T(8,128)}, u32[]{:S(2)}, u32[]{:S(2)}) %collective-permute-start.8) | collective-permute-done | bytes 524320 | tf_op jit(solution)/shard_map/ppermute | solution.py:11
  67.2 7.9 %collective-permute-done.1 = f32[8,128,128]{2,1,0:T(8,128)S(1)} collective-permute-done((f32[8,128,128]{2,1,0:T(8,128)S(1)}, f32[8,128,128]{2,1,0:T(8,128)S(1)}, u32[]{:S(2)}, u32[]{:S(2)}) %collective-permute-start.1) | collective-permute-done | bytes 524320 | tf_op jit(solution)/shard_map/ppermute | solution.py:11
  76.8 3.0 %collective-permute-start.10 = (f32[8,128,128]{2,1,0:T(8,128)S(1)}, f32[8,128,128]{2,1,0:T(8,128)S(1)}, u32[]{:S(2)}, u32[]{:S(2)}) collective-permute-start(f32[8,128,128]{2,1,0:T(8,128)S(1)} %add.180), channel_id=1, source_target_pairs={{0,16},{2,18},{4,20},{6,22},{8,24},{10,26},{12,28},{14,30},{16,0},... | collective-permute-start | bytes 1572872 | tf_op jit(solution)/shard_map/ppermute | solution.py:11
  82.4 6.9 %collective-permute-done.2 = f32[8,128,128]{2,1,0:T(8,128)S(1)} collective-permute-done((f32[8,128,128]{2,1,0:T(8,128)S(1)}, f32[8,128,128]{2,1,0:T(8,128)S(1)}, u32[]{:S(2)}, u32[]{:S(2)}) %collective-permute-start.2) | collective-permute-done | bytes 524320 | tf_op jit(solution)/shard_map/ppermute | solution.py:11
  91.0 2.9 %collective-permute-start.3 = (f32[8,128,128]{2,1,0:T(8,128)}, f32[8,128,128]{2,1,0:T(8,128)}, u32[]{:S(2)}, u32[]{:S(2)}) collective-permute-start(f32[8,128,128]{2,1,0:T(8,128)} %add.160), channel_id=1, source_target_pairs={{0,16},{2,18},{4,20},{6,22},{8,24},{10,26},{12,28},{14,30},{16,0},... | collective-permute-start | bytes 1572872 | tf_op jit(solution)/shard_map/ppermute | solution.py:11
  93.9 9.1 %collective-permute-done.10 = f32[8,128,128]{2,1,0:T(8,128)S(1)} collective-permute-done((f32[8,128,128]{2,1,0:T(8,128)S(1)}, f32[8,128,128]{2,1,0:T(8,128)S(1)}, u32[]{:S(2)}, u32[]{:S(2)}) %collective-permute-start.10) | collective-permute-done | bytes 524320 | tf_op jit(solution)/shard_map/ppermute | solution.py:11
  104.6 1.6 collective-permute-start.11
  106.2 1.5 pad_add_fusion
  107.7 2.9 %copy.102 = f32[2,2,8,128,128]{3,4,2,1,0:T(8,128)} copy(f32[2,2,8,128,128]{4,3,2,0,1:T(8,128)} %pad_add_fusion) | data formatting | bytes 4194304 | tf_op jit(solution)/shard_map/add | solution.py:32
  110.7 1.7 pad_add_fusion.1
  112.4 1.5 copy.91
  115.6 1.7 collective-permute-start.4
  118.5 3.2 %collective-permute-start.12 = (f32[8,128,128]{2,1,0:T(8,128)S(1)}, f32[8,128,128]{2,1,0:T(8,128)S(1)}, u32[]{:S(2)}, u32[]{:S(2)}) collective-permute-start(f32[8,128,128]{2,1,0:T(8,128)S(1)} %add.184), channel_id=1, source_target_pairs={{0,64},{2,66},{4,68},{6,70},{8,72},{10,74},{12,76},{14,78},{16,80}... | collective-permute-start | bytes 1572872 | tf_op jit(solution)/shard_map/ppermute | solution.py:11
  122.7 1.9 fusion.12
  124.5 12.8 %collective-permute-done.4 = f32[8,128,128]{2,1,0:T(8,128)S(1)} collective-permute-done((f32[8,128,128]{2,1,0:T(8,128)S(1)}, f32[8,128,128]{2,1,0:T(8,128)S(1)}, u32[]{:S(2)}, u32[]{:S(2)}) %collective-permute-start.4) | collective-permute-done | bytes 524320 | tf_op jit(solution)/shard_map/ppermute | solution.py:11
  139.0 1.7 collective-permute-start.5
  142.3 5.3 %collective-permute-start.13 = (f32[8,128,128]{2,1,0:T(8,128)}, f32[8,128,128]{2,1,0:T(8,128)}, u32[]{:S(2)}, u32[]{:S(2)}) collective-permute-start(f32[8,128,128]{2,1,0:T(8,128)} %add.186), channel_id=1, source_target_pairs={{0,128},{2,130},{4,132},{6,134},{8,136},{10,138},{12,140},{14,142}... | collective-permute-start | bytes 1572872 | tf_op jit(solution)/shard_map/ppermute | solution.py:11
  147.7 1.7 fusion.22
  149.4 2.6 fusion.3
  151.9 26.1 %collective-permute-done.5 = f32[8,128,128]{2,1,0:T(8,128)} collective-permute-done((f32[8,128,128]{2,1,0:T(8,128)}, f32[8,128,128]{2,1,0:T(8,128)}, u32[]{:S(2)}, u32[]{:S(2)}) %collective-permute-start.5) | collective-permute-done | bytes 524320 | tf_op jit(solution)/shard_map/ppermute | solution.py:11
  178.1 2.1 add.169
  180.2 13.8 %collective-permute-start.6 = (f32[8,128,128]{2,1,0:T(8,128)}, f32[8,128,128]{2,1,0:T(8,128)}, u32[]{:S(2)}, u32[]{:S(2)}) collective-permute-start(f32[8,128,128]{2,1,0:T(8,128)} %add.169), channel_id=1, source_target_pairs={{0,128},{2,130},{4,132},{6,134},{8,136},{10,138},{12,140},{14,142}... | collective-permute-start | bytes 1572872 | tf_op jit(solution)/shard_map/ppermute | solution.py:11
  194.0 2.3 multiply_add_fusion
  197.3 2.1 bitcast_add_fusion.2
  199.7 2.3 fusion
  204.0 33.7 %all_to_all.121 = bf16[2,256,1024]{2,1,0:T(8,128)(2,1)} all-to-all(bf16[2,256,1024]{2,1,0:T(8,128)(2,1)} %all_to_all.110), channel_id=1, replica_groups=mesh['seq'=128,'head'=2] {'head'}, dimensions={0} | all-to-all | bytes 2097152 | tf_op jit(solution)/shard_map/all_to_all | solution.py:153
  237.7 2.3 copy.116
  240.0 2.3 copy.119
  242.3 2.9 %fusion.1 = bf16[4,128,8,128]{3,1,2,0:T(8,128)(2,1)S(1)} fusion(f32[4,8,128,128]{3,2,1,0:T(8,128)} %fusion.12, f32[4,8,128,128]{2,3,1,0:T(8,128)S(1)} %bitcast_add_fusion.2, bf16[4,128,8,128]{3,2,1,0:T(8,128)(2,1)S(1)} %bitcast.110), kind=kOutput, calls=%fused_computation.3 | convolution fusion | flops 806354944 | bytes 6291456 | tf_op jit(solution)/shard_map/nshe,nhde->nshd/dot_general | solution.py:105
  246.4 4.7 %all_to_all.122 = bf16[2,256,1024]{2,1,0:T(8,128)(2,1)S(1)} all-to-all(bf16[2,256,1024]{2,1,0:T(8,128)(2,1)S(1)} %all_to_all.106), channel_id=1, replica_groups=mesh['seq'=128,'head'=2] {'head'}, dimensions={0} | all-to-all | bytes 2097152 | tf_op jit(solution)/shard_map/all_to_all | solution.py:152
  253.1 2.0 multiply_add_fusion.1
  257.2 2.3 fusion.2
  260.7 4.5 %all_to_all.123 = bf16[2,256,1024]{2,1,0:T(8,128)(2,1)S(1)} all-to-all(bf16[2,256,1024]{2,1,0:T(8,128)(2,1)S(1)} %all_to_all.99), channel_id=1, replica_groups=mesh['seq'=128,'head'=2] {'head'}, dimensions={0} | all-to-all | bytes 2097152 | tf_op jit(solution)/shard_map/all_to_all | solution.py:151
  (97 shorter events, 36.9 us)
Async XLA Ops:
  0.6 9.2 %copy-start.20 = (bf16[256,2048]{1,0:T(8,128)(2,1)S(1)}, bf16[256,2048]{1,0:T(8,128)(2,1)}, u32[]{:S(2)}) copy-start(bf16[256,2048]{1,0:T(8,128)(2,1)} %param.5) | copy-start | bytes 3145732
  3.0 8.6 %all-to-all-start = ((bf16[256,2,1024]{2,0,1:T(8,128)(2,1)}), bf16[256,2,1024]{2,0,1:T(8,128)(2,1)S(1)}, u32[]{:S(2)}, u32[]{:S(2)}) async-start(bf16[256,2,1024]{2,0,1:T(8,128)(2,1)} %bitcast.96), calls=%async_computation | async-start | bytes 2097152 | tf_op jit(solution)/shard_map/all_to_all | solution.py:130
  11.6 5.7 %all-to-all-start.4 = ((bf16[256,2,1024]{2,0,1:T(8,128)(2,1)}), bf16[256,2,1024]{2,0,1:T(8,128)(2,1)S(1)}, u32[]{:S(2)}, u32[]{:S(2)}) async-start(bf16[256,2,1024]{2,0,1:T(8,128)(2,1)} %bitcast.93), calls=%async_computation.4 | async-start | bytes 2097152 | tf_op jit(solution)/shard_map/all_to_all | solution.py:127
  15.8 133.6 %copy-start = (bf16[64,8,8,128]{3,2,1,0:T(8,128)(2,1)}, bf16[64,8,8,128]{3,2,1,0:T(8,128)(2,1)S(1)}, u32[]{:S(2)}) copy-start(bf16[64,8,8,128]{3,2,1,0:T(8,128)(2,1)S(1)} %copy.131) | copy-start | bytes 3145732
  17.5 2.7 %copy-start.21 = (bf16[256,2048]{1,0:T(8,128)(2,1)S(1)}, bf16[256,2048]{1,0:T(8,128)(2,1)}, u32[]{:S(2)}) copy-start(bf16[256,2048]{1,0:T(8,128)(2,1)} %param.6) | copy-start | bytes 3145732
  20.2 19.5 %collective-permute-start.7 = (f32[8,128,128]{2,1,0:T(8,128)}, f32[8,128,128]{2,1,0:T(8,128)}, u32[]{:S(2)}, u32[]{:S(2)}) collective-permute-start(f32[8,128,128]{2,1,0:T(8,128)} %get-tuple-element.32), channel_id=1, source_target_pairs={{0,2},{2,0},{4,6},{6,4},{8,10},{10,8},{12,14},{14,12},{16,18},{18,... | collective-permute-start | bytes 1572872 | tf_op jit(solution)/shard_map/ppermute | solution.py:11
  21.3 6.2 %all-to-all-start.2 = ((bf16[256,2,1024]{2,0,1:T(8,128)(2,1)}), bf16[256,2,1024]{2,0,1:T(8,128)(2,1)S(1)}, u32[]{:S(2)}, u32[]{:S(2)}) async-start(bf16[256,2,1024]{2,0,1:T(8,128)(2,1)} %bitcast.119), calls=%async_computation.2 | async-start | bytes 2097152 | tf_op jit(solution)/shard_map/all_to_all | solution.py:128
  27.5 4.4 %copy-start.10 = (bf16[256,2,1024]{2,0,1:T(8,128)(2,1)}, bf16[256,2,1024]{2,0,1:T(8,128)(2,1)S(1)}, u32[]{:S(2)}) copy-start(bf16[256,2,1024]{2,0,1:T(8,128)(2,1)S(1)} %all-to-all-done.2) | copy-start | bytes 3145732
  27.5 6.3 %all-to-all-start.1 = ((bf16[256,2,1024]{2,0,1:T(8,128)(2,1)}), bf16[256,2,1024]{2,0,1:T(8,128)(2,1)}, u32[]{:S(2)}, u32[]{:S(2)}) async-start(bf16[256,2,1024]{2,0,1:T(8,128)(2,1)} %bitcast.118), calls=%async_computation.1 | async-start | bytes 2097152 | tf_op jit(solution)/shard_map/all_to_all | solution.py:129
  35.3 2.7 copy-start.2
  38.0 6.3 %copy-start.22 = (f32[16,11]{1,0:T(8,128)S(1)}, f32[16,11]{1,0:T(8,128)}, u32[]{:S(2)}) copy-start(f32[16,11]{1,0:T(8,128)} %param.9) | copy-start | bytes 2116
  38.0 14.1 %collective-permute-start = (f32[8,128,128]{2,1,0:T(8,128)}, f32[8,128,128]{2,1,0:T(8,128)}, u32[]{:S(2)}, u32[]{:S(2)}) collective-permute-start(f32[8,128,128]{2,1,0:T(8,128)} %get-tuple-element.30), channel_id=1, source_target_pairs={{0,2},{2,0},{4,6},{6,4},{8,10},{10,8},{12,14},{14,12},{16,18},{18,... | collective-permute-start | bytes 1572872 | tf_op jit(solution)/shard_map/ppermute | solution.py:11
  41.8 22.2 %collective-permute-start.8 = (f32[8,128,128]{2,1,0:T(8,128)}, f32[8,128,128]{2,1,0:T(8,128)}, u32[]{:S(2)}, u32[]{:S(2)}) collective-permute-start(f32[8,128,128]{2,1,0:T(8,128)} %add.176), channel_id=1, source_target_pairs={{0,4},{2,6},{4,0},{6,2},{8,12},{10,14},{12,8},{14,10},{16,20},{18,... | collective-permute-start | bytes 1572872 | tf_op jit(solution)/shard_map/ppermute | solution.py:11
  42.8 24.1 %copy-start.8 = (f32[4,8,128,128]{3,2,1,0:T(8,128)S(1)}, f32[4,8,128,128]{3,2,1,0:T(8,128)}, u32[]{:S(2)}) copy-start(f32[4,8,128,128]{3,2,1,0:T(8,128)} %get-tuple-element.31) | copy-start | bytes 6291460
  53.3 21.8 %collective-permute-start.1 = (f32[8,128,128]{2,1,0:T(8,128)S(1)}, f32[8,128,128]{2,1,0:T(8,128)S(1)}, u32[]{:S(2)}, u32[]{:S(2)}) collective-permute-start(f32[8,128,128]{2,1,0:T(8,128)S(1)} %add.154), channel_id=1, source_target_pairs={{0,4},{2,6},{4,0},{6,2},{8,12},{10,14},{12,8},{14,10},{16,20},{18,... | collective-permute-start | bytes 1572872 | tf_op jit(solution)/shard_map/ppermute | solution.py:11
  65.2 11.5 %collective-permute-start.9 = (f32[8,128,128]{2,1,0:T(8,128)S(1)}, f32[8,128,128]{2,1,0:T(8,128)S(1)}, u32[]{:S(2)}, u32[]{:S(2)}) collective-permute-start(f32[8,128,128]{2,1,0:T(8,128)S(1)} %add.178), channel_id=1, source_target_pairs={{0,8},{2,10},{4,12},{6,14},{8,0},{10,2},{12,4},{14,6},{16,24},{18,... | collective-permute-start | bytes 1572872 | tf_op jit(solution)/shard_map/ppermute | solution.py:11
  75.1 6.1 %copy-start.11 = (f32[8,128,128]{2,1,0:T(8,128)}, f32[8,128,128]{2,1,0:T(8,128)S(1)}, u32[]{:S(2)}) copy-start(f32[8,128,128]{2,1,0:T(8,128)S(1)} %collective-permute-done.1) | copy-start | bytes 1572868
  75.2 6.0 %copy-start.7 = (f32[4,8,128,128]{3,2,1,0:T(8,128)S(1)}, f32[4,8,128,128]{3,2,1,0:T(8,128)}, u32[]{:S(2)}) copy-start(f32[4,8,128,128]{3,2,1,0:T(8,128)} %get-tuple-element.33) | copy-start | bytes 6291460
  75.2 14.1 %collective-permute-start.2 = (f32[8,128,128]{2,1,0:T(8,128)S(1)}, f32[8,128,128]{2,1,0:T(8,128)S(1)}, u32[]{:S(2)}, u32[]{:S(2)}) collective-permute-start(f32[8,128,128]{2,1,0:T(8,128)S(1)} %add.157), channel_id=1, source_target_pairs={{0,8},{2,10},{4,12},{6,14},{8,0},{10,2},{12,4},{14,6},{16,24},{18,... | collective-permute-start | bytes 1572872 | tf_op jit(solution)/shard_map/ppermute | solution.py:11
  76.7 3.4 %copy-start.15 = (f32[8,128,128]{2,1,0:T(8,128)}, f32[8,128,128]{2,1,0:T(8,128)S(1)}, u32[]{:S(2)}) copy-start(f32[8,128,128]{2,1,0:T(8,128)S(1)} %collective-permute-done.9) | copy-start | bytes 1572868
  76.8 26.2 %collective-permute-start.10 = (f32[8,128,128]{2,1,0:T(8,128)S(1)}, f32[8,128,128]{2,1,0:T(8,128)S(1)}, u32[]{:S(2)}, u32[]{:S(2)}) collective-permute-start(f32[8,128,128]{2,1,0:T(8,128)S(1)} %add.180), channel_id=1, source_target_pairs={{0,16},{2,18},{4,20},{6,22},{8,24},{10,26},{12,28},{14,30},{16,0},... | collective-permute-start | bytes 1572872 | tf_op jit(solution)/shard_map/ppermute | solution.py:11
  89.3 0.8 copy-start.13
  91.0 23.3 %collective-permute-start.3 = (f32[8,128,128]{2,1,0:T(8,128)}, f32[8,128,128]{2,1,0:T(8,128)}, u32[]{:S(2)}, u32[]{:S(2)}) collective-permute-start(f32[8,128,128]{2,1,0:T(8,128)} %add.160), channel_id=1, source_target_pairs={{0,16},{2,18},{4,20},{6,22},{8,24},{10,26},{12,28},{14,30},{16,0},... | collective-permute-start | bytes 1572872 | tf_op jit(solution)/shard_map/ppermute | solution.py:11
  103.0 0.8 copy-start.16
  104.6 12.7 %collective-permute-start.11 = (f32[8,128,128]{2,1,0:T(8,128)}, f32[8,128,128]{2,1,0:T(8,128)}, u32[]{:S(2)}, u32[]{:S(2)}) collective-permute-start(f32[8,128,128]{2,1,0:T(8,128)} %add.182), channel_id=1, source_target_pairs={{0,32},{2,34},{4,36},{6,38},{8,40},{10,42},{12,44},{14,46},{16,48}... | collective-permute-start | bytes 1572872 | tf_op jit(solution)/shard_map/ppermute | solution.py:11
  113.9 7.9 %copy-start.3 = (bf16[64,8,8,128]{3,2,1,0:T(8,128)(2,1)S(1)}, bf16[64,8,8,128]{3,2,1,0:T(8,128)(2,1)}, u32[]{:S(2)}) copy-start(bf16[64,8,8,128]{3,2,1,0:T(8,128)(2,1)} %copy-done.2) | copy-start | bytes 3145732
  115.6 21.8 %collective-permute-start.4 = (f32[8,128,128]{2,1,0:T(8,128)S(1)}, f32[8,128,128]{2,1,0:T(8,128)S(1)}, u32[]{:S(2)}, u32[]{:S(2)}) collective-permute-start(f32[8,128,128]{2,1,0:T(8,128)S(1)} %add.163), channel_id=1, source_target_pairs={{0,32},{2,34},{4,36},{6,38},{8,40},{10,42},{12,44},{14,46},{16,48}... | collective-permute-start | bytes 1572872 | tf_op jit(solution)/shard_map/ppermute | solution.py:11
  118.5 22.1 %collective-permute-start.12 = (f32[8,128,128]{2,1,0:T(8,128)S(1)}, f32[8,128,128]{2,1,0:T(8,128)S(1)}, u32[]{:S(2)}, u32[]{:S(2)}) collective-permute-start(f32[8,128,128]{2,1,0:T(8,128)S(1)} %add.184), channel_id=1, source_target_pairs={{0,64},{2,66},{4,68},{6,70},{8,72},{10,74},{12,76},{14,78},{16,80}... | collective-permute-start | bytes 1572872 | tf_op jit(solution)/shard_map/ppermute | solution.py:11
  137.3 0.8 copy-start.17
  139.0 39.1 %collective-permute-start.5 = (f32[8,128,128]{2,1,0:T(8,128)}, f32[8,128,128]{2,1,0:T(8,128)}, u32[]{:S(2)}, u32[]{:S(2)}) collective-permute-start(f32[8,128,128]{2,1,0:T(8,128)} %add.166), channel_id=1, source_target_pairs={{0,64},{2,66},{4,68},{6,70},{8,72},{10,74},{12,76},{14,78},{16,80}... | collective-permute-start | bytes 1572872 | tf_op jit(solution)/shard_map/ppermute | solution.py:11
  140.7 0.8 copy-start.19
  142.3 51.7 %collective-permute-start.13 = (f32[8,128,128]{2,1,0:T(8,128)}, f32[8,128,128]{2,1,0:T(8,128)}, u32[]{:S(2)}, u32[]{:S(2)}) collective-permute-start(f32[8,128,128]{2,1,0:T(8,128)} %add.186), channel_id=1, source_target_pairs={{0,128},{2,130},{4,132},{6,134},{8,136},{10,138},{12,140},{14,142}... | collective-permute-start | bytes 1572872 | tf_op jit(solution)/shard_map/ppermute | solution.py:11
  180.2 72.9 %collective-permute-start.6 = (f32[8,128,128]{2,1,0:T(8,128)}, f32[8,128,128]{2,1,0:T(8,128)}, u32[]{:S(2)}, u32[]{:S(2)}) collective-permute-start(f32[8,128,128]{2,1,0:T(8,128)} %add.169), channel_id=1, source_target_pairs={{0,128},{2,130},{4,132},{6,134},{8,136},{10,138},{12,140},{14,142}... | collective-permute-start | bytes 1572872 | tf_op jit(solution)/shard_map/ppermute | solution.py:11
  197.3 2.4 copy-start.6
  237.7 4.6 %copy-start.4 = (bf16[64,8,8,128]{3,2,1,0:T(8,128)(2,1)S(1)}, bf16[64,8,8,128]{3,2,1,0:T(8,128)(2,1)}, u32[]{:S(2)}) copy-start(bf16[64,8,8,128]{3,2,1,0:T(8,128)(2,1)} %copy-done.2) | copy-start | bytes 3145732
  251.1 2.0 copy-start.12
  251.1 2.0 copy-start.14
  251.6 1.4 copy-start.18
  253.1 2.2 copy-start.9
  255.3 1.2 copy-start.1
  255.3 1.9 copy-start.5
where the time goes:
time: 268 us; the launch traced here: 267 us
  waiting for transfers between devices  82.6 us (31%)
  starting transfers between devices  59.7 us (22%)
  blocking collectives  42.8 us (16%)
  local copies, waits for them, and re-layouts  35.1 us (13%)
  other arithmetic  26.1 us (10%)
  matrix products  19.9 us (7%)
    ppermute x14, waiting for transfers between devices, partner(): lax.ppermute(array, axis, [(i, i ^ 1 << distance) for i in range(lax.axis...  80.1 us
    ppermute x14, starting transfers between devices, partner(): lax.ppermute(array, axis, [(i, i ^ 1 << distance) for i in range(lax.axis...  40.6 us
    all_to_all x1, blocking collectives, body(): lax.all_to_all(value_part, 'head', split_axis=0, concat_axis=1, tiled=True)  33.7 us
    unnamed x53, local copies, waits for them, and re-layouts  14.1 us
    all_to_all x1, starting transfers between devices, body(): lax.all_to_all(out_grad, 'head', split_axis=1, concat_axis=0, tiled=True)  6.81 us
    add x6, other arithmetic, cross_states(): group_kv = group_kv + other_kv  6.39 us
    add x6, other arithmetic, cross_states(): group_qo = group_qo + other_qo  6.31 us
  transfers between devices with their start and end apart: 18, of which 12 were waited for; matrix products, arithmetic and copies ran while one was open for 23% of the time, Pallas kernels for 0%

commit v1 on v0

v1 whole, which is shorter than its diff:
```python
import functools

import jax
import jax.numpy as jnp
from jax import lax
from jax.experimental import pallas as pl
from jax.experimental.pallas import tpu as pltpu
from jax.sharding import PartitionSpec as P

DH = 128
BLOCK = 128
NX, NY, NZ = 4, 4, 8
PLANE = NX * NY
HEADS = 16
OWN = HEADS // 2
HALF = DH // 2
TOK = 256
MESH = pl.DeviceIdType.MESH
PRE = float(2.0**40)
POST = float(2.0**-40)
LEVEL_C = [float(2.0 ** ((1.0 - l) / 2.0) / 128.0) for l in range(11)]


def encode(x):
    s = x * PRE
    return (s * jnp.abs(s)).astype(jnp.bfloat16)


def decode(y):
    y = y.astype(jnp.float32)
    return y * (lax.rsqrt(jnp.maximum(jnp.abs(y), 1e-37)) * POST)


def dot_nn(a, b):
    return lax.dot_general(a, b, (((1,), (0,)), ((), ())), preferred_element_type=jnp.float32)


def dot_nt(a, b):
    return lax.dot_general(a, b, (((1,), (1,)), ((), ())), preferred_element_type=jnp.float32)


def dot_tn(a, b):
    return lax.dot_general(a, b, (((0,), (0,)), ((), ())), preferred_element_type=jnp.float32)


def split(x):
    hi = x.astype(jnp.bfloat16)
    lo = (x - hi.astype(jnp.float32)).astype(jnp.bfloat16)
    return hi, lo


def kernel(
    lw, q_hbm, k_hbm, v_hbm, o_hbm, qg_hbm, kg_hbm, vg_hbm,
    qs, ks, vs, os_, sums, kv0, qo1, from_core, from_core_x,
    send1, recv1, zsend, zrecv, send3, recv3, fwd3, plane_buf, part_q, part_k, part_v,
    out_q, out_k, out_v,
    in_sem, d_send, d_recv, x_send, x_recv, s1_send, s1_recv, z_send, z_recv,
    s3_send, s3_recv, f_send, f_recv, out_sem,
):
    seq = lax.axis_index("seq")
    core = lax.axis_index("head")
    x = lax.rem(seq, NX)
    y = lax.rem(lax.div(seq, NX), NY)
    z = lax.div(seq, PLANE)
    me = y * NX + x
    pair = lax.div(me, 2)
    sibling = (seq, 1 - core)

    def chip(i):
        return (z * PLANE + i, core)

    loads = []
    for n, (src, dst) in enumerate(((k_hbm, ks), (v_hbm, vs), (q_hbm, qs), (o_hbm, os_))):
        c = pltpu.make_async_copy(src, dst, in_sem.at[n])
        c.start()
        loads.append(c)

    barrier = pltpu.get_barrier_semaphore()
    pl.semaphore_signal(barrier, inc=1, device_id=sibling, device_id_type=MESH)
    for d in range(1, PLANE):
        pl.semaphore_signal(
            barrier, inc=1, device_id=chip(lax.rem(me + d, PLANE)), device_id_type=MESH
        )
    for d in range(1, NZ):
        pl.semaphore_signal(
            barrier,
            inc=1,
            device_id=(lax.rem(z + d, NZ) * PLANE + me, core),
            device_id_type=MESH,
        )
    pl.semaphore_wait(barrier, 1 + PLANE - 1 + NZ - 1)
    for c in loads:
        c.wait()

    def cols(h):
        return pl.ds(pl.multiple_of(h * DH, DH), DH)

    def states(h):
        c = cols(h)
        kv_a = dot_tn(vs[0:BLOCK, c], ks[0:BLOCK, c])
        kv_b = dot_tn(vs[BLOCK:TOK, c], ks[BLOCK:TOK, c])
        qo_a = dot_tn(qs[0:BLOCK, c], os_[0:BLOCK, c])
        qo_b = dot_tn(qs[BLOCK:TOK, c], os_[BLOCK:TOK, c])
        kv0[h] = kv_a
        qo1[h] = qo_b
        return kv_a + kv_b, qo_a + qo_b

    def to_core(j):
        return pltpu.make_async_remote_copy(
            src_ref=sums.at[(1 - core) * OWN + j],
            dst_ref=from_core.at[j],
            send_sem=d_send.at[j],
            recv_sem=d_recv.at[j],
            device_id=sibling,
            device_id_type=MESH,
        )

    def order(r):
        return lax.rem(pair + 1 + r, OWN)

    def first(r, _):
        j = order(r)
        h = (1 - core) * OWN + j
        kv, qo = states(h)
        sums[h, 0] = kv
        sums[h, 1] = qo
        to_core(j).start()
        return 0

    lax.fori_loop(0, OWN, first, 0)

    def plane_copy(i):
        return pltpu.make_async_remote_copy(
            src_ref=send1.at[i],
            dst_ref=recv1.at[me],
            send_sem=s1_send.at[i],
            recv_sem=s1_recv.at[me],
            device_id=chip(i),
            device_id_type=MESH,
        )

    def second(r, _):
        j = order(r)
        h = core * OWN + j
        kv, qo = states(h)
        sums[h, 0] = kv
        sums[h, 1] = qo
        to_core(j).wait_recv()
        for half in range(2):
            rows = slice(half * HALF, (half + 1) * HALF)
            i = 2 * j + half
            send1[i, 0] = encode(kv[rows] + from_core[j, 0, rows])
            send1[i, 1] = encode(qo[rows] + from_core[j, 1, rows])

            @pl.when(i != me)
            def _():
                plane_copy(i).start()

        return 0

    lax.fori_loop(0, OWN, second, 0)
    recv1[me] = send1[me]

    extra = pltpu.make_async_remote_copy(
        src_ref=sums.at[pl.ds(core * OWN, OWN), core],
        dst_ref=from_core_x,
        send_sem=x_send,
        recv_sem=x_recv,
        device_id=sibling,
        device_id_type=MESH,
    )
    extra.start()

    row = lax.broadcasted_iota(jnp.int32, (BLOCK, BLOCK), 0)
    col = lax.broadcasted_iota(jnp.int32, (BLOCK, BLOCK), 1)
    lower = row >= col
    upper = row <= col

    def local(h, _):
        c = cols(h)
        w0 = lw[h, 0] * LEVEL_C[0]
        w1 = lw[h, 1] * LEVEL_C[1]
        for b in range(2):
            rows = slice(b * BLOCK, (b + 1) * BLOCK)
            qb, kb, vb, ob = qs[rows, c], ks[rows, c], vs[rows, c], os_[rows, c]
            w_t = jnp.where(upper, dot_nt(kb, qb) * w0, 0.0).astype(jnp.bfloat16)
            g_t = jnp.where(upper, dot_nt(vb, ob) * w0, 0.0).astype(jnp.bfloat16)
            g = jnp.where(lower, dot_nt(ob, vb) * w0, 0.0).astype(jnp.bfloat16)
            ql = dot_nn(g, kb)
            kl = dot_nn(g_t, qb)
            vl = dot_nn(w_t, ob)
            if b == 1:
                hi, lo = split(kv0[h] * w1)
                ql = ql + (dot_nn(ob, hi) + dot_nn(ob, lo))
            else:
                hi, lo = split(qo1[h] * w1)
                kl = kl + (dot_nt(vb, hi) + dot_nt(vb, lo))
                vl = vl + (dot_nn(kb, hi) + dot_nn(kb, lo))
            part_q[rows, c] = ql
            part_k[rows, c] = kl
            part_v[rows, c] = vl
        return 0

    lax.fori_loop(0, HEADS, local, 0)

    hs = core * OWN + pair

    def weight(level):
        return lw[hs, level] * LEVEL_C[level]

    def plane_wait(i):
        return pltpu.make_async_remote_copy(
            src_ref=send1.at[i],
            dst_ref=recv1.at[i],
            send_sem=s1_send.at[i],
            recv_sem=s1_recv.at[i],
            device_id=chip(i),
            device_id_type=MESH,
        )

    def wait_plane(d, _):
        plane_wait(lax.rem(me + d, PLANE)).wait_recv()
        return 0

    lax.fori_loop(1, PLANE, wait_plane, 0)

    for kind in range(2):
        nodes = [decode(recv1[i, kind]) for i in range(PLANE)]
        tree = [nodes]
        while len(tree[-1]) > 1:
            last = tree[-1]
            tree.append([last[n] + last[n + 1] for n in range(0, len(last), 2)])
        zsend[kind] = encode(tree[-1][0])
        down = [None]
        for level in range(len(tree) - 2, -1, -1):
            w = weight(3 + level)
            new = []
            for n, parent in enumerate(down):
                a, b = tree[level][2 * n], tree[level][2 * n + 1]
                from_a, from_b = parent, parent
                if kind == 0:
                    from_b = a * w if parent is None else parent + a * w
                else:
                    from_a = b * w if parent is None else parent + b * w
                new += [from_a, from_b]
            down = new
        for i in range(PLANE):
            value = down[i]
            plane_buf[i, kind] = jnp.zeros((HALF, DH), jnp.float32) if value is None else value

    def z_copy(d):
        other = lax.rem(z + d, NZ)
        which = lax.select(other > z, 0, 1)
        return pltpu.make_async_remote_copy(
            src_ref=zsend.at[which],
            dst_ref=zrecv.at[d - 1],
            send_sem=z_send.at[d - 1],
            recv_sem=z_recv.at[d - 1],
            device_id=(other * PLANE + me, core),
            device_id_type=MESH,
        )

    z_copies = [z_copy(d) for d in range(1, NZ)]
    for c in z_copies:
        c.start()
    z_e = jnp.zeros((HALF, DH), jnp.float32)
    z_l = jnp.zeros((HALF, DH), jnp.float32)
    for d in range(1, NZ):
        z_copies[d - 1].wait_recv()
        src = lax.rem(z + NZ - d, NZ)
        diff = src ^ z
        w = lax.select(diff >= 4, weight(9), lax.select(diff >= 2, weight(8), weight(7)))
        value = decode(zrecv[d - 1]) * w
        z_e = z_e + lax.select(src < z, 1.0, 0.0) * value
        z_l = z_l + lax.select(src < z, 0.0, 1.0) * value

    def back_copy(i):
        return pltpu.make_async_remote_copy(
            src_ref=send3.at[i],
            dst_ref=recv3.at[me],
            send_sem=s3_send.at[i],
            recv_sem=s3_recv.at[me],
            device_id=chip(i),
            device_id_type=MESH,
        )

    for d in range(1, PLANE + 1):
        i = lax.rem(me + d, PLANE)
        send3[i, 0] = encode(plane_buf[i, 0] + z_e)
        send3[i, 1] = encode(plane_buf[i, 1] + z_l)
        if d < PLANE:
            back_copy(i).start()
        else:
            recv3[i] = send3[i]

    def back_wait(i):
        return pltpu.make_async_remote_copy(
            src_ref=send3.at[i],
            dst_ref=recv3.at[i],
            send_sem=s3_send.at[i],
            recv_sem=s3_recv.at[i],
            device_id=chip(i),
            device_id_type=MESH,
        )

    def forward(i):
        return pltpu.make_async_remote_copy(
            src_ref=recv3.at[i],
            dst_ref=fwd3.at[i],
            send_sem=f_send.at[i],
            recv_sem=f_recv.at[i],
            device_id=sibling,
            device_id_type=MESH,
        )

    extra.wait_recv()
    up = lax.select(core == 1, 1.0, 0.0)
    dn = 1.0 - up

    def stores(h):
        c = cols(h)
        return [
            pltpu.make_async_copy(s.at[:, c], t.at[:, c], out_sem.at[n, h])
            for n, (s, t) in enumerate(((out_q, qg_hbm), (out_k, kg_hbm), (out_v, vg_hbm)))
        ]

    def finish(h, cross_e, cross_l):
        c = cols(h)
        e_hi, e_lo = split(cross_e)
        l_hi, l_lo = split(cross_l)
        ob, vb, kb = os_[:, c], vs[:, c], ks[:, c]
        out_q[:, c] = (part_q[:, c] + (dot_nn(ob, e_hi) + dot_nn(ob, e_lo))).astype(jnp.bfloat16)
        out_k[:, c] = (part_k[:, c] + (dot_nt(vb, l_hi) + dot_nt(vb, l_lo))).astype(jnp.bfloat16)
        out_v[:, c] = (part_v[:, c] + (dot_nn(kb, l_hi) + dot_nn(kb, l_lo))).astype(jnp.bfloat16)
        for s in stores(h):
            s.start()

    def whole(buf, j, kind):
        return decode(jnp.concatenate([buf[2 * j, kind], buf[2 * j + 1, kind]], axis=0))

    def own_head(r, _):
        j = lax.rem(pair + r, OWN)
        for half in range(2):
            i = 2 * j + half

            @pl.when(i != me)
            def _():
                back_wait(i).wait_recv()

            forward(i).start()
        h = core * OWN + j
        w2 = lw[h, 2] * LEVEL_C[2]
        finish(
            h,
            whole(recv3, j, 0) + (w2 * up) * from_core[j, 0],
            whole(recv3, j, 1) + (w2 * dn) * from_core[j, 1],
        )
        return 0

    lax.fori_loop(0, OWN, own_head, 0)

    def other_head(r, _):
        j = lax.rem(pair + r, OWN)
        for half in range(2):
            forward(2 * j + half).wait_recv()
        h = (1 - core) * OWN + j
        w2 = lw[h, 2] * LEVEL_C[2]
        finish(
            h,
            whole(fwd3, j, 0) + (w2 * up) * from_core_x[j],
            whole(fwd3, j, 1) + (w2 * dn) * from_core_x[j],
        )
        return 0

    lax.fori_loop(0, OWN, other_head, 0)

    def drain_core(j, _):
        to_core(j).wait_send()
        return 0

    lax.fori_loop(0, OWN, drain_core, 0)
    extra.wait_send()
    for c in z_copies:
        c.wait_send()

    def drain_plane(d, _):
        i = lax.rem(me + d, PLANE)
        plane_copy(i).wait_send()
        back_copy(i).wait_send()
        return 0

    lax.fori_loop(1, PLANE, drain_plane, 0)

    def drain_forward(i, _):
        forward(i).wait_send()
        return 0

    lax.fori_loop(0, PLANE, drain_forward, 0)

    def drain_out(h, _):
        for s in stores(h):
            s.wait()
        return 0

    lax.fori_loop(0, HEADS, drain_out, 0)


def body(queries, key_rows, values, out_grad, level_weights):
    any_spec = pl.BlockSpec(memory_space=pl.ANY)
    bf, f32 = jnp.bfloat16, jnp.float32
    dma = pltpu.SemaphoreType.DMA
    rows = (TOK, HEADS * DH)
    out = jax.ShapeDtypeStruct(rows, bf)
    return tuple(
        pl.pallas_call(
            kernel,
            name="fenwick",
            out_shape=(out, out, out),
            in_specs=[pl.BlockSpec(memory_space=pltpu.SMEM)] + [any_spec] * 4,
            out_specs=(any_spec,) * 3,
            scratch_shapes=[pltpu.VMEM(rows, bf)] * 4
            + [
                pltpu.VMEM((HEADS, 2, DH, DH), f32),
                pltpu.VMEM((HEADS, DH, DH), f32),
                pltpu.VMEM((HEADS, DH, DH), f32),
                pltpu.VMEM((OWN, 2, DH, DH), f32),
                pltpu.VMEM((OWN, DH, DH), f32),
                pltpu.VMEM((PLANE, 2, HALF, DH), bf),
                pltpu.VMEM((PLANE, 2, HALF, DH), bf),
                pltpu.VMEM((2, HALF, DH), bf),
                pltpu.VMEM((NZ - 1, HALF, DH), bf),
                pltpu.VMEM((PLANE, 2, HALF, DH), bf),
                pltpu.VMEM((PLANE, 2, HALF, DH), bf),
                pltpu.VMEM((PLANE, 2, HALF, DH), bf),
                pltpu.VMEM((PLANE, 2, HALF, DH), f32),
            ]
            + [pltpu.VMEM(rows, f32)] * 3
            + [pltpu.VMEM(rows, bf)] * 3
            + [
                dma((4,)),
                dma((OWN,)),
                dma((OWN,)),
                dma,
                dma,
                dma((PLANE,)),
                dma((PLANE,)),
                dma((NZ - 1,)),
                dma((NZ - 1,)),
                dma((PLANE,)),
                dma((PLANE,)),
                dma((PLANE,)),
                dma((PLANE,)),
                dma((3, HEADS)),
            ],
            compiler_params=pltpu.CompilerParams(
                collective_id=0, has_side_effects=True, vmem_limit_bytes=48 << 20
            ),
        )(level_weights, queries, key_rows, values, out_grad)
    )


def solution(mesh):
    rows = P(("seq", "head"), None)
    return jax.shard_map(
        body,
        mesh=mesh,
        in_specs=(rows, rows, rows, rows, P()),
        out_specs=(rows, rows, rows),
        check_vma=False,
    )
```

time: 268 us -> 50.6 us (0.19)
  waiting for transfers between devices: 82.6 us -> 0 us
  starting transfers between devices: 59.7 us -> 0 us
  Pallas kernels: 0 us -> 43.7 us
  blocking collectives: 42.8 us -> 0 us
  local copies, waits for them, and re-layouts: 35.1 us -> 6.05 us
  other arithmetic: 26.1 us -> 0 us
  matrix products: 19.9 us -> 0 us
    ppermute x14 -> x0, waiting for transfers between devices: 80.1 us -> none  [partner(): lax.ppermute(array, axis, [(i, i ^ 1 << distance) for i in range(lax.axis...]
    pallas_call x0 -> x1, Pallas kernels: none -> 43.7 us  [body(): pl.pallas_call(kernel, name='fenwick', out_shape=(out, out, out), in_spec...]
    all_to_all x3 -> x0, blocking collectives: 42.8 us -> none  [the longest x1 33.7 us: body(): lax.all_to_all(value_part, 'head', split_axis=0, concat_axis=1, tiled=True)]
    ppermute x14 -> x0, starting transfers between devices: 40.6 us -> none  [partner(): lax.ppermute(array, axis, [(i, i ^ 1 << distance) for i in range(lax.axis...]
    add x18 -> x0, other arithmetic: 22.5 us -> none  [the longest x6 6.39 us: cross_states(): group_kv = group_kv + other_kv]
    dot_general x9 -> x0, matrix products: 19.9 us -> none  [the longest x1 2.93 us: range_grads(): jnp.einsum('nshe,nhde->nshd', value_blk, later, precision=high, preferred...]
    all_to_all x4 -> x0, starting transfers between devices: 19.1 us -> none  [the longest x1 6.81 us: body(): lax.all_to_all(out_grad, 'head', split_axis=1, concat_axis=0, tiled=True)]
    all_to_all x10 -> x0, local copies, waits for them, and re-layouts: 12.4 us -> none  [the longest x2 3.62 us: body(): lax.all_to_all(value_part, 'head', split_axis=0, concat_axis=1, tiled=True)]
  transfers between devices with their start and end apart: 18 -> 0, of which waited for: 12 -> 0; matrix products, arithmetic and copies ran while one was open for 23% -> 0% of each run, Pallas kernels for 0% -> 0%
where the time goes in v1:
time: 50.6 us; the launch traced here: 50.4 us
  Pallas kernels  43.7 us (86%)
  local copies, waits for them, and re-layouts  6.05 us (12%)
  between operations  0.65 us (1%)
    pallas_call x1, Pallas kernels, body(): pl.pallas_call(kernel, name='fenwick', out_shape=(out, out, out), in_spec...  43.7 us
    unnamed x9, local copies, waits for them, and re-layouts  6.05 us

profile of v1, /device:TPU:1, one launch (start us, length us, event | category | flops | bytes accessed | tf_op | source)
XLA Modules:
  0.0 50.4 jit_solution(17431563573521742920)
XLA Ops:
  0.6 0.0 copy-start
  0.6 1.2 %copy-done = bf16[256,2048]{1,0:T(8,128)(2,1)S(1)} copy-done((bf16[256,2048]{1,0:T(8,128)(2,1)S(1)}, bf16[256,2048]{1,0:T(8,128)(2,1)}, u32[]{:S(2)}) %copy-start) | copy-done | bytes 1048600
  1.9 0.0 copy-start.1
  1.9 1.2 %copy-done.1 = bf16[256,2048]{1,0:T(8,128)(2,1)S(1)} copy-done((bf16[256,2048]{1,0:T(8,128)(2,1)S(1)}, bf16[256,2048]{1,0:T(8,128)(2,1)}, u32[]{:S(2)}) %copy-start.1) | copy-done | bytes 1048600
  3.1 0.0 copy-start.2
  3.1 0.7 %copy-done.2 = f32[16,11]{1,0:T(8,128)S(1)} copy-done((f32[16,11]{1,0:T(8,128)S(1)}, f32[16,11]{1,0:T(8,128)}, u32[]{:S(2)}) %copy-start.2) | copy-done | bytes 728
  3.8 43.7 %fenwick.1 = (bf16[256,2048]{1,0:T(8,128)(2,1)S(1)}, bf16[256,2048]{1,0:T(8,128)(2,1)S(1)}, bf16[256,2048]{1,0:T(8,128)(2,1)S(1)}) custom-call(f32[16,11]{1,0:T(8,128)S(1)} %copy-done.2, bf16[256,2048]{1,0:T(8,128)(2,1)S(1)} %copy-done, bf16[256,2048]{1,0:T(8,128)(2,1)S(1)} %copy-done.1, bf16[256,2048]{1,0:T(8,128)(2,1)} %v_hbm.1, bf16[256,2048]{1,0:T(8,128)(2,1)} %o_hbm.1), custom_call_target="tpu_custom_call" | custom-call | tf_op jit(solution)/shard_map/fenwick/pallas_call | solution.py:415
  47.5 1.0 %copy.11 = bf16[256,2048]{1,0:T(8,128)(2,1)} copy(bf16[256,2048]{1,0:T(8,128)(2,1)S(1)} %get-tuple-element.6) | data formatting | bytes 2097152
  48.4 1.0 %copy.12 = bf16[256,2048]{1,0:T(8,128)(2,1)} copy(bf16[256,2048]{1,0:T(8,128)(2,1)S(1)} %get-tuple-element.7) | data formatting | bytes 2097152
  49.4 1.0 %copy.13 = bf16[256,2048]{1,0:T(8,128)(2,1)} copy(bf16[256,2048]{1,0:T(8,128)(2,1)S(1)} %get-tuple-element.8) | data formatting | bytes 2097152
Async XLA Ops:
  0.6 1.2 %copy-start = (bf16[256,2048]{1,0:T(8,128)(2,1)S(1)}, bf16[256,2048]{1,0:T(8,128)(2,1)}, u32[]{:S(2)}) copy-start(bf16[256,2048]{1,0:T(8,128)(2,1)} %q_hbm.1) | copy-start | bytes 3145732
  1.9 1.2 %copy-start.1 = (bf16[256,2048]{1,0:T(8,128)(2,1)S(1)}, bf16[256,2048]{1,0:T(8,128)(2,1)}, u32[]{:S(2)}) copy-start(bf16[256,2048]{1,0:T(8,128)(2,1)} %k_hbm.1) | copy-start | bytes 3145732
  3.1 0.7 %copy-start.2 = (f32[16,11]{1,0:T(8,128)S(1)}, f32[16,11]{1,0:T(8,128)}, u32[]{:S(2)}) copy-start(f32[16,11]{1,0:T(8,128)} %lw.1) | copy-start | bytes 2116

commit v2 on v0

v2 whole, which is shorter than its diff:
```python
import functools

import jax
import jax.numpy as jnp
from jax import lax
from jax.experimental import pallas as pl
from jax.experimental.pallas import tpu as pltpu
from jax.sharding import PartitionSpec as P

DH = 128
BLOCK = 128
NX, NY, NZ = 4, 4, 8
PLANE = NX * NY
HEADS = 16
OWN = HEADS // 2
HALF = DH // 2
TOK = 256
MESH = pl.DeviceIdType.MESH
GROUP = 4
LOCAL_GROUP = 2
SPLIT_A = 4
LOAD_PARTS = 2
STORE_PARTS = 4
PRE = float(2.0**40)
POST = float(2.0**-40)
LEVEL_C = [float(2.0 ** ((1.0 - l) / 2.0) / 128.0) for l in range(11)]


def encode(x):
    s = x * PRE
    return (s * jnp.abs(s)).astype(jnp.bfloat16)


def decode(y):
    y = y.astype(jnp.float32)
    return y * (lax.rsqrt(jnp.maximum(jnp.abs(y), 1e-37)) * POST)


def dot_nn(a, b):
    return lax.dot_general(a, b, (((1,), (0,)), ((), ())), preferred_element_type=jnp.float32)


def dot_nt(a, b):
    return lax.dot_general(a, b, (((1,), (1,)), ((), ())), preferred_element_type=jnp.float32)


def dot_tn(a, b):
    return lax.dot_general(a, b, (((0,), (0,)), ((), ())), preferred_element_type=jnp.float32)


def split(x):
    hi = x.astype(jnp.bfloat16)
    lo = (x - hi.astype(jnp.float32)).astype(jnp.bfloat16)
    return hi, lo


def kernel(
    lw_hbm, q_hbm, k_hbm, v_hbm, o_hbm, out_q, out_k, out_v,
    lw, qs, ks, vs, os_, sums, to_sibling, to_extra, from_core, from_core_x,
    send1, recv1, zsend, zrecv, z_total, send3, recv3, fwd3, plane_buf, part_q, part_k, part_v,
    in_sem, d_send, d_recv, x_send, x_recv, z_ready, s1_send, s1_recv, z_send, z_recv,
    s3_send, s3_recv, f_send, f_recv,
):
    seq = lax.axis_index("seq")
    core = lax.axis_index("head")
    x = lax.rem(seq, NX)
    y = lax.rem(lax.div(seq, NX), NY)
    z = lax.div(seq, PLANE)
    me = y * NX + x
    pair = lax.div(me, 2)
    sibling = (seq, 1 - core)

    def chip(i):
        return (z * PLANE + i, core)

    width = OWN * DH
    loads = []
    stages = [(arrays, owner) for arrays in ("qo", "kv") for owner in (1 - core, core)]
    where = dict(q=(q_hbm, qs), k=(k_hbm, ks), v=(v_hbm, vs), o=(o_hbm, os_))
    for n, (arrays, owner) in enumerate(stages):
        half = pl.ds(pl.multiple_of(owner * width, width), width)
        loads.append([])
        for array in arrays:
            src, dst = where[array]
            for p in range(LOAD_PARTS):
                rows = pl.ds(p * (TOK // LOAD_PARTS), TOK // LOAD_PARTS)
                loads[n].append(
                    pltpu.make_async_copy(src.at[rows, half], dst.at[rows, half], in_sem.at[n])
                )
    loads.append([pltpu.make_async_copy(lw_hbm, lw, in_sem.at[4])])

    def start_loads(lo, hi):
        for stage in loads[lo:hi]:
            for c in stage:
                c.start()

    def wait_loads(n):
        if n < 4:
            drain(qs, in_sem.at[n])
        else:
            loads[n][0].wait()

    start_loads(0, 2)
    barrier = pltpu.get_barrier_semaphore()
    pl.semaphore_signal(barrier, inc=1, device_id=sibling, device_id_type=MESH)
    for d in range(1, PLANE):
        pl.semaphore_signal(
            barrier, inc=1, device_id=chip(lax.rem(me + d, PLANE)), device_id_type=MESH
        )
    for d in range(1, NZ):
        other = lax.rem(z + d, NZ)

        @pl.when(other > z)
        def _():
            pl.semaphore_signal(
                barrier, inc=1, device_id=(other * PLANE + me, core), device_id_type=MESH
            )

    def wait_barrier():
        pl.semaphore_wait(barrier, PLANE + z)
        for d in range(1, NZ):
            other = lax.rem(z + d, NZ)

            @pl.when(other < z)
            def _():
                pl.semaphore_signal(
                    z_ready, inc=1, device_id=(other * PLANE + me, core), device_id_type=MESH
                )

    start_loads(2, 5)

    def drain(buf, sem):
        pltpu.make_async_copy(buf, buf, sem).wait()

    def cols(h):
        return pl.ds(pl.multiple_of(h * DH, DH), DH)

    def states(kind, h):
        a, b = (vs, ks) if kind == 0 else (qs, os_)
        c = cols(h)
        return dot_tn(a[:, c], b[:, c])

    def part(j):
        return lax.div(lax.rem(j - pair - 1 + 2 * OWN, OWN), GROUP)

    def to_core(kind, j):
        return pltpu.make_async_remote_copy(
            src_ref=to_sibling.at[kind, j],
            dst_ref=from_core.at[kind, j],
            send_sem=d_send.at[kind],
            recv_sem=d_recv.at[kind, part(j)],
            device_id=sibling,
            device_id_type=MESH,
        )

    def order(r):
        return lax.rem(pair + 1 + r, OWN)

    def group(g):
        return [order(g * GROUP + n) for n in range(GROUP)]

    def states_for_sibling(kind, g):
        values = [states(kind, (1 - core) * OWN + j) for j in group(g)]
        for j, value in zip(group(g), values):
            to_sibling[kind, j] = encode(value)

    def send_core(kind, g):
        for j in group(g):
            to_core(kind, j).start()

    def states_own(kind, g):
        values = [states(kind, core * OWN + j) for j in group(g)]
        for j, value in zip(group(g), values):
            sums[kind, j] = value

    def plane_copy(kind, i):
        return pltpu.make_async_remote_copy(
            src_ref=send1.at[kind, i],
            dst_ref=recv1.at[kind, me],
            send_sem=s1_send.at[kind],
            recv_sem=s1_recv.at[kind],
            device_id=chip(i),
            device_id_type=MESH,
        )

    def send_plane(kind, g):
        drain(from_core.at[kind, pl.ds(0, GROUP)], d_recv.at[kind, g])
        for j in group(g):
            for half in range(2):
                rows = pl.ds(half * HALF, HALF)
                total = sums[kind, j, rows] + decode(from_core[kind, j, rows])
                send1[kind, 2 * j + half] = encode(total)
        for j in group(g):
            for half in range(2):
                i = 2 * j + half

                @pl.when(i != me)
                def _():
                    plane_copy(kind, i).start()

    def keep_plane(kind):
        recv1[kind, me] = send1[kind, me]

    wait_loads(0)
    states_for_sibling(1, 0)
    wait_barrier()
    send_core(1, 0)
    states_for_sibling(1, 1)
    send_core(1, 1)
    wait_loads(1)
    states_own(1, 0)
    states_own(1, 1)
    send_plane(1, 0)
    send_plane(1, 1)
    keep_plane(1)
    wait_loads(2)
    states_for_sibling(0, 0)
    send_core(0, 0)
    states_for_sibling(0, 1)
    send_core(0, 1)
    wait_loads(3)
    states_own(0, 0)
    states_own(0, 1)
    wait_loads(4)

    row = lax.broadcasted_iota(jnp.int32, (BLOCK, BLOCK), 0)
    col = lax.broadcasted_iota(jnp.int32, (BLOCK, BLOCK), 1)
    lower = row >= col
    upper = row <= col

    A, B = slice(0, BLOCK), slice(BLOCK, TOK)

    def local_heads(first_head):
        heads = [first_head + n for n in range(LOCAL_GROUP)]
        data = []
        for h in heads:
            c = cols(h)
            data.append((qs[:, c], ks[:, c], vs[:, c], os_[:, c]))
        scores = []
        for qb, kb, vb, ob in data:
            scores.append(
                (
                    dot_nt(ob[A], vb[A]), dot_nt(ob[B], vb),
                    dot_nt(vb[A], ob), dot_nt(vb[B], ob[B]),
                    dot_nt(kb[A], qb), dot_nt(kb[B], qb[B]),
                )
            )
        weighted = []
        for h, (g_a, g_b, gt_a, gt_b, wt_a, wt_b) in zip(heads, scores):
            w0 = lw[h, 0] * LEVEL_C[0]
            w1 = lw[h, 1] * LEVEL_C[1]

            def masked(score, mask):
                return jnp.where(mask, score * w0, 0.0).astype(jnp.bfloat16)

            def level1(score):
                return (score * w1).astype(jnp.bfloat16)

            def join(a, b):
                return jnp.concatenate([a, b], axis=1)

            weighted.append(
                (
                    masked(g_a, lower), join(level1(g_b[:, A]), masked(g_b[:, B], lower)),
                    join(masked(gt_a[:, A], upper), level1(gt_a[:, B])), masked(gt_b, upper),
                    join(masked(wt_a[:, A], upper), level1(wt_a[:, B])), masked(wt_b, upper),
                )
            )
        results = []
        for (qb, kb, vb, ob), (g_a, g_b, gt_a, gt_b, wt_a, wt_b) in zip(data, weighted):
            results.append(
                (
                    dot_nn(g_a, kb[A]), dot_nn(g_b, kb),
                    dot_nn(gt_a, qb), dot_nn(gt_b, qb[B]),
                    dot_nn(wt_a, ob), dot_nn(wt_b, ob[B]),
                )
            )
        for h, values in zip(heads, results):
            c = cols(h)
            for n, part in enumerate((part_q, part_k, part_v)):
                part[A, c] = values[2 * n]
                part[B, c] = values[2 * n + 1]

    def local(lo, hi):
        def step(n, _):
            local_heads(lo + n * LOCAL_GROUP)
            return 0

        lax.fori_loop(0, (hi - lo) // LOCAL_GROUP, step, 0)

    extra = pltpu.make_async_remote_copy(
        src_ref=to_extra,
        dst_ref=from_core_x,
        send_sem=x_send,
        recv_sem=x_recv,
        device_id=sibling,
        device_id_type=MESH,
    )

    hs = core * OWN + pair

    def weight(level):
        return lw[hs, level] * LEVEL_C[level]

    def combine(kind):
        others = pl.ds(0, PLANE - 1)
        pltpu.make_async_copy(
            recv1.at[kind, others], recv1.at[kind, others], s1_recv.at[kind]
        ).wait()
        nodes = [decode(recv1[kind, i]) for i in range(PLANE)]
        tree = [nodes]
        while len(tree[-1]) > 1:
            last = tree[-1]
            tree.append([last[n] + last[n + 1] for n in range(0, len(last), 2)])
        zsend[kind] = encode(tree[-1][0])
        if kind == 0:

            @pl.when(z < NZ - 1)
            def _():
                pl.semaphore_wait(z_ready, NZ - 1 - z)

        for d in range(1, NZ):

            @pl.when(z_sends(kind, d))
            def _():
                z_copy(kind, d).start()

        down = [None]
        for level in range(len(tree) - 2, -1, -1):
            w = weight(3 + level)
            new = []
            for n, parent in enumerate(down):
                a, b = tree[level][2 * n], tree[level][2 * n + 1]
                from_a, from_b = parent, parent
                if kind == 0:
                    from_b = a * w if parent is None else parent + a * w
                else:
                    from_a = b * w if parent is None else parent + b * w
                new += [from_a, from_b]
            down = new
        for i in range(PLANE):
            value = down[i]
            plane_buf[kind, i] = jnp.zeros((HALF, DH), jnp.float32) if value is None else value

    def z_sends(kind, d):
        other = lax.rem(z + d, NZ)
        return other > z if kind == 0 else other < z

    def z_takes(kind, d):
        src = lax.rem(z + NZ - d, NZ)
        return src < z if kind == 0 else src > z

    def z_copy(kind, d):
        return pltpu.make_async_remote_copy(
            src_ref=zsend.at[kind],
            dst_ref=zrecv.at[d - 1],
            send_sem=z_send,
            recv_sem=z_recv.at[d - 1],
            device_id=(lax.rem(z + d, NZ) * PLANE + me, core),
            device_id_type=MESH,
        )

    def back_part(chip_pair, from_pair):
        return lax.div(lax.rem(from_pair - chip_pair + OWN, OWN), GROUP)

    def back_copy(kind, i):
        return pltpu.make_async_remote_copy(
            src_ref=send3.at[kind, i],
            dst_ref=recv3.at[kind, me],
            send_sem=s3_send.at[kind],
            recv_sem=s3_recv.at[kind, back_part(lax.div(i, 2), pair)],
            device_id=chip(i),
            device_id_type=MESH,
        )

    def give_back(kind):
        for d in range(1, NZ):

            @pl.when(z_takes(kind, d))
            def _():
                z_copy(kind, d).wait_recv()

        z_total[...] = jnp.zeros((HALF, DH), jnp.float32)
        for d in range(1, NZ):

            @pl.when(z_takes(kind, d))
            def _():
                diff = lax.rem(z + NZ - d, NZ) ^ z
                w = lax.select(diff >= 4, weight(9), lax.select(diff >= 2, weight(8), weight(7)))
                z_total[...] = z_total[...] + decode(zrecv[d - 1]) * w

        total = z_total[...]

        def step(d, _):
            i = lax.rem(me + d, PLANE)
            send3[kind, i] = encode(plane_buf[kind, i] + total)
            back_copy(kind, i).start()
            return 0

        lax.fori_loop(1, PLANE, step, 0, unroll=3)
        recv3[kind, me] = encode(plane_buf[kind, me] + total)

    def start_extra():
        def step(j, _):
            to_extra[j] = encode(sums[core, j])
            return 0

        lax.fori_loop(0, OWN, step, 0)
        extra.start()

    low = z < NZ // 2
    high = z >= NZ // 2

    def in_order(step):
        @pl.when(low)
        def _():
            step(0)
            step(1)

        @pl.when(high)
        def _():
            step(1)
            step(0)

    local(0, SPLIT_A)
    send_plane(0, 0)
    send_plane(0, 1)
    keep_plane(0)
    start_extra()
    local(SPLIT_A, HEADS)
    combine(1)
    combine(0)
    in_order(give_back)

    def forward(kind, j):
        slots = pl.ds(2 * j, 2)
        return pltpu.make_async_remote_copy(
            src_ref=recv3.at[kind, slots],
            dst_ref=fwd3.at[kind, slots],
            send_sem=f_send.at[kind],
            recv_sem=f_recv.at[kind, back_part(pair, j)],
            device_id=sibling,
            device_id_type=MESH,
        )

    def drain_early():
        extra.wait_send()
        drain(zrecv, z_send)
        for kind in range(2):
            drain(to_sibling.at[kind], d_send.at[kind])
            drain(send1.at[kind, pl.ds(0, PLANE - 1)], s1_send.at[kind])

    drain_early()
    extra.wait_recv()
    up = lax.select(core == 1, 1.0, 0.0)
    dn = 1.0 - up

    def finish(kind, heads, crosses):
        values = []
        for h, cross in zip(heads, crosses):
            c = cols(h)
            hi, lo = split(cross)
            stack = jnp.concatenate([hi, lo], axis=0)
            if kind == 0:
                ob = os_[:, c]
                more = dot_nn(jnp.concatenate([ob, ob], axis=1), stack)
                values.append((out_q, c, part_q[:, c] + more))
            else:
                vb, kb = vs[:, c], ks[:, c]
                wide = jnp.concatenate([hi, lo], axis=1)
                more = dot_nt(jnp.concatenate([vb, vb], axis=1), wide)
                values.append((out_k, c, part_k[:, c] + more))
                more = dot_nn(jnp.concatenate([kb, kb], axis=1), stack)
                values.append((out_v, c, part_v[:, c] + more))
        for ref, c, value in values:
            ref[:, c] = value.astype(jnp.bfloat16)

    def whole(buf, kind, j):
        return decode(jnp.concatenate([buf[kind, 2 * j], buf[kind, 2 * j + 1]], axis=0))

    def level2(kind, h):
        return lw[h, 2] * LEVEL_C[2] * (up if kind == 0 else dn)

    def back_group(g):
        return [lax.rem(pair + g * GROUP + n, OWN) for n in range(GROUP)]

    def pass_on(kind):
        for g in range(OWN // GROUP):
            slots = 2 * GROUP - (1 if g == 0 else 0)
            drain(recv3.at[kind, pl.ds(0, slots)], s3_recv.at[kind, g])
            for j in back_group(g):
                forward(kind, j).start()

    def own_heads(kind):
        def step(g, _):
            slots = back_group(g)
            heads = [core * OWN + j for j in slots]
            finish(
                kind,
                heads,
                [
                    whole(recv3, kind, j) + level2(kind, h) * decode(from_core[kind, j])
                    for j, h in zip(slots, heads)
                ],
            )
            return 0

        lax.fori_loop(0, OWN // GROUP, step, 0)

    def other_heads(kind):
        for g in range(OWN // GROUP):
            slots = back_group(g)
            drain(fwd3.at[kind, pl.ds(0, 2 * GROUP)], f_recv.at[kind, g])
            heads = [(1 - core) * OWN + j for j in slots]
            finish(
                kind,
                heads,
                [
                    whole(fwd3, kind, j) + level2(kind, h) * decode(from_core_x[j])
                    for j, h in zip(slots, heads)
                ],
            )

    def drain_late():
        for kind in range(2):
            drain(send3.at[kind, pl.ds(0, PLANE - 1)], s3_send.at[kind])
            drain(fwd3.at[kind], f_send.at[kind])

    def finish_all(kind):
        pass_on(kind)
        own_heads(kind)
        other_heads(kind)

    in_order(finish_all)
    drain_late()


def store(a, b, c, x, y, z, sem):
    part = TOK // STORE_PARTS
    copies = []
    for n, (src, dst) in enumerate(((a, x), (b, y), (c, z))):
        for p in range(STORE_PARTS):
            rows = pl.ds(p * part, part)
            copies.append(pltpu.make_async_copy(src.at[rows], dst.at[rows], sem.at[n, p]))
    for copy in copies:
        copy.start()
    for copy in copies:
        copy.wait()


def body(queries, key_rows, values, out_grad, level_weights):
    any_spec = pl.BlockSpec(memory_space=pl.ANY)
    hbm = pl.BlockSpec(memory_space=pltpu.HBM)
    vmem = pl.BlockSpec(memory_space=pltpu.VMEM)
    bf, f32 = jnp.bfloat16, jnp.float32
    dma = pltpu.SemaphoreType.DMA
    rows = (TOK, HEADS * DH)
    out = jax.ShapeDtypeStruct(rows, bf)
    pinned = [
        pltpu.with_memory_space_constraint(a, pltpu.HBM)
        for a in (level_weights, queries, key_rows, values, out_grad)
    ]
    grads = pl.pallas_call(
        kernel,
        name="fenwick",
        out_shape=(pltpu.VMEM(rows, bf),) * 3,
        in_specs=[hbm] * 5,
        out_specs=(vmem,) * 3,
        scratch_shapes=[pltpu.SMEM((HEADS, 11), f32)]
        + [pltpu.VMEM(rows, bf)] * 4
        + [
            pltpu.VMEM((2, OWN, DH, DH), f32),
            pltpu.VMEM((2, OWN, DH, DH), bf),
            pltpu.VMEM((OWN, DH, DH), bf),
            pltpu.VMEM((2, OWN, DH, DH), bf),
            pltpu.VMEM((OWN, DH, DH), bf),
            pltpu.VMEM((2, PLANE, HALF, DH), bf),
            pltpu.VMEM((2, PLANE, HALF, DH), bf),
            pltpu.VMEM((2, HALF, DH), bf),
            pltpu.VMEM((NZ - 1, HALF, DH), bf),
            pltpu.VMEM((HALF, DH), f32),
            pltpu.VMEM((2, PLANE, HALF, DH), bf),
            pltpu.VMEM((2, PLANE, HALF, DH), bf),
            pltpu.VMEM((2, PLANE, HALF, DH), bf),
            pltpu.VMEM((2, PLANE, HALF, DH), f32),
        ]
        + [pltpu.VMEM(rows, f32)] * 3
        + [
            dma((5,)),
            dma((2,)),
            dma((2, OWN // GROUP)),
            dma,
            dma,
            pltpu.SemaphoreType.REGULAR,
            dma((2,)),
            dma((2,)),
            dma,
            dma((NZ - 1,)),
            dma((2,)),
            dma((2, OWN // GROUP)),
            dma((2,)),
            dma((2, OWN // GROUP)),
        ],
        compiler_params=pltpu.CompilerParams(
            collective_id=0, has_side_effects=True, vmem_limit_bytes=40 << 20
        ),
    )(*pinned)
    return tuple(
        pl.pallas_call(
            store,
            name="store",
            out_shape=(out, out, out),
            in_specs=[any_spec] * 3,
            out_specs=(hbm,) * 3,
            scratch_shapes=[dma((3, STORE_PARTS))],
        )(*(pltpu.with_memory_space_constraint(g, pltpu.VMEM) for g in grads))
    )


def solution(mesh):
    rows = P(("seq", "head"), None)
    return jax.shard_map(
        body,
        mesh=mesh,
        in_specs=(rows, rows, rows, rows, P()),
        out_specs=(rows, rows, rows),
        check_vma=False,
    )
```

time: 268 us -> 33.7 us (0.13)
  waiting for transfers between devices: 82.6 us -> 0 us
  starting transfers between devices: 59.7 us -> 0 us
  blocking collectives: 42.8 us -> 0 us
  local copies, waits for them, and re-layouts: 35.1 us -> 0 us
  Pallas kernels: 0 us -> 32.9 us
  other arithmetic: 26.1 us -> 0 us
  matrix products: 19.9 us -> 0 us
    ppermute x14 -> x0, waiting for transfers between devices: 80.1 us -> none  [partner(): lax.ppermute(array, axis, [(i, i ^ 1 << distance) for i in range(lax.axis...]
    all_to_all x3 -> x0, blocking collectives: 42.8 us -> none  [the longest x1 33.7 us: body(): lax.all_to_all(value_part, 'head', split_axis=0, concat_axis=1, tiled=True)]
    ppermute x14 -> x0, starting transfers between devices: 40.6 us -> none  [partner(): lax.ppermute(array, axis, [(i, i ^ 1 << distance) for i in range(lax.axis...]
    pallas_call x0 -> x2, Pallas kernels: none -> 32.9 us  [the longest x1 31.2 us: body(): pl.pallas_call(kernel, name='fenwick', out_shape=(pltpu.VMEM(rows, bf),)...]
    add x18 -> x0, other arithmetic: 22.5 us -> none  [the longest x6 6.39 us: cross_states(): group_kv = group_kv + other_kv]
    dot_general x9 -> x0, matrix products: 19.9 us -> none  [the longest x1 2.93 us: range_grads(): jnp.einsum('nshe,nhde->nshd', value_blk, later, precision=high, preferred...]
    all_to_all x4 -> x0, starting transfers between devices: 19.1 us -> none  [the longest x1 6.81 us: body(): lax.all_to_all(out_grad, 'head', split_axis=1, concat_axis=0, tiled=True)]
    unnamed x53 -> x0, local copies, waits for them, and re-layouts: 14.1 us -> none
  transfers between devices with their start and end apart: 18 -> 0, of which waited for: 12 -> 0; matrix products, arithmetic and copies ran while one was open for 23% -> 0% of each run, Pallas kernels for 0% -> 0%
where the time goes in v2:
time: 33.7 us; the launch traced here: 33.6 us
  Pallas kernels  32.9 us (98%)
  between operations  0.64 us (2%)
    pallas_call x1, Pallas kernels, body(): pl.pallas_call(kernel, name='fenwick', out_shape=(pltpu.VMEM(rows, bf),)...  31.2 us
    pallas_call x1, Pallas kernels, body(): pl.pallas_call(store, name='store', out_shape=(out, out, out), in_specs=[...  1.76 us

profile of v2, /device:TPU:1, one launch (start us, length us, event | category | flops | bytes accessed | tf_op | source)
XLA Modules:
  0.0 33.6 jit_solution(12112841922323241862)
XLA Ops:
  0.6 31.2 %fenwick.1 = (bf16[256,2048]{1,0:T(8,128)(2,1)S(1)}, bf16[256,2048]{1,0:T(8,128)(2,1)S(1)}, bf16[256,2048]{1,0:T(8,128)(2,1)S(1)}) custom-call(f32[16,11]{1,0:T(8,128)} %lw_hbm.1, bf16[256,2048]{1,0:T(8,128)(2,1)} %q_hbm.1, bf16[256,2048]{1,0:T(8,128)(2,1)} %k_hbm.1, bf16[256,2048]{1,0:T(8,128)(2,1)} %v_hbm.1, bf16[256,2048]{1,0:T(8,128)(2,1)} %o_hbm.1), custom_call_target="tpu_custom_call" | custom-call | tf_op jit(solution)/shard_map/fenwick/pallas_call | solution.py:563
  31.8 1.8 %store.1 = (bf16[256,2048]{1,0:T(8,128)(2,1)}, bf16[256,2048]{1,0:T(8,128)(2,1)}, bf16[256,2048]{1,0:T(8,128)(2,1)}) custom-call(bf16[256,2048]{1,0:T(8,128)(2,1)S(1)} %get-tuple-element.6.a, bf16[256,2048]{1,0:T(8,128)(2,1)S(1)} %get-tuple-element.7.b, bf16[256,2048]{1,0:T(8,128)(2,1)S(1)} %get-tuple-element.8.c), custom_call_target="tpu_custom_call" | custom-call | tf_op jit(solution)/shard_map/store/pallas_call | solution.py:609

commit v3 on v2

--- a/solution.py
+++ b/solution.py
@@ -11,6 +11,9 @@
 BLOCK = 128
 NX, NY, NZ = 4, 4, 8
 PLANE = NX * NY
+BACK_ORDER = sorted(
+    range(PLANE), key=lambda i: (min(i % NX, NX - i % NX) + min(i // NX, NY - i // NX), i)
+)
 HEADS = 16
 OWN = HEADS // 2
 HALF = DH // 2
@@ -18,7 +21,7 @@
 MESH = pl.DeviceIdType.MESH
 GROUP = 4
 LOCAL_GROUP = 2
-SPLIT_A = 4
+SPLIT_A, SPLIT_B = 10, 10
 LOAD_PARTS = 2
 STORE_PARTS = 4
 PRE = float(2.0**40)
@@ -55,9 +58,10 @@
 
 
 def kernel(
-    lw_hbm, q_hbm, k_hbm, v_hbm, o_hbm, out_q, out_k, out_v,
-    lw, qs, ks, vs, os_, sums, to_sibling, to_extra, from_core, from_core_x,
-    send1, recv1, zsend, zrecv, z_total, send3, recv3, fwd3, plane_buf, part_q, part_k, part_v,
+    lw_hbm, q_hbm, k_hbm, v_hbm, o_hbm,
+    out_q, out_k, out_v, fwd3, base_x, part_k, part_v, ks, vs,
+    lw, qs, os_, sums, to_sibling, to_extra, from_core, from_core_x,
+    send1, recv1, zsend, zrecv, z_total, send3, recv3, plane_buf, part_q,
     in_sem, d_send, d_recv, x_send, x_recv, z_ready, s1_send, s1_recv, z_send, z_recv,
     s3_send, s3_recv, f_send, f_recv,
 ):
@@ -100,10 +104,9 @@
         else:
             loads[n][0].wait()
 
-    start_loads(0, 2)
     barrier = pltpu.get_barrier_semaphore()
     pl.semaphore_signal(barrier, inc=1, device_id=sibling, device_id_type=MESH)
-    for d in range(1, PLANE):
+    for d in (10, 6, 9, 11, 14, 2, 8, 5, 7, 13, 15, 1, 3, 4, 12):
         pl.semaphore_signal(
             barrier, inc=1, device_id=chip(lax.rem(me + d, PLANE)), device_id_type=MESH
         )
@@ -116,6 +119,8 @@
                 barrier, inc=1, device_id=(other * PLANE + me, core), device_id_type=MESH
             )
 
+    start_loads(0, 2)
+
     def wait_barrier():
         pl.semaphore_wait(barrier, PLANE + z)
         for d in range(1, NZ):
@@ -126,8 +131,6 @@
                 pl.semaphore_signal(
                     z_ready, inc=1, device_id=(other * PLANE + me, core), device_id_type=MESH
                 )
-
-    start_loads(2, 5)
 
     def drain(buf, sem):
         pltpu.make_async_copy(buf, buf, sem).wait()
@@ -202,13 +205,14 @@
         recv1[kind, me] = send1[kind, me]
 
     wait_loads(0)
+    start_loads(2, 5)
     states_for_sibling(1, 0)
+    states_for_sibling(1, 1)
+    wait_loads(1)
+    states_own(1, 0)
     wait_barrier()
     send_core(1, 0)
-    states_for_sibling(1, 1)
     send_core(1, 1)
-    wait_loads(1)
-    states_own(1, 0)
     states_own(1, 1)
     send_plane(1, 0)
     send_plane(1, 1)
@@ -391,14 +395,14 @@
 
         total = z_total[...]
 
-        def step(d, _):
-            i = lax.rem(me + d, PLANE)
+        for i in BACK_ORDER:
             send3[kind, i] = encode(plane_buf[kind, i] + total)
-            back_copy(kind, i).start()
-            return 0
-
-        lax.fori_loop(1, PLANE, step, 0, unroll=3)
-        recv3[kind, me] = encode(plane_buf[kind, me] + total)
+
+            @pl.when(i != me)
+            def _():
+                back_copy(kind, i).start()
+
+        recv3[kind, me] = send3[kind, me]
 
     def start_extra():
         def step(j, _):
@@ -427,8 +431,9 @@
     send_plane(0, 1)
     keep_plane(0)
     start_extra()
-    local(SPLIT_A, HEADS)
+    local(SPLIT_A, SPLIT_B)
     combine(1)
+    local(SPLIT_B, HEADS)
     combine(0)
     in_order(give_back)
 
@@ -451,10 +456,22 @@
             drain(send1.at[kind, pl.ds(0, PLANE - 1)], s1_send.at[kind])
 
     drain_early()
-    extra.wait_recv()
     up = lax.select(core == 1, 1.0, 0.0)
     dn = 1.0 - up
 
+    def level2(kind, h):
+        return lw[h, 2] * LEVEL_C[2] * (up if kind == 0 else dn)
+
+    def make_base():
+        def step(j, _):
+            h = (1 - core) * OWN + j
+            base_x[j] = level2(1, h) * decode(from_core_x[j])
+            return 0
+
+        lax.fori_loop(0, OWN, step, 0)
+
+    extra.wait_recv()
+    make_base()
     def finish(kind, heads, crosses):
         values = []
         for h, cross in zip(heads, crosses):
@@ -478,9 +495,6 @@
     def whole(buf, kind, j):
         return decode(jnp.concatenate([buf[kind, 2 * j], buf[kind, 2 * j + 1]], axis=0))
 
-    def level2(kind, h):
-        return lw[h, 2] * LEVEL_C[2] * (up if kind == 0 else dn)
-
     def back_group(g):
         return [lax.rem(pair + g * GROUP + n, OWN) for n in range(GROUP)]
 
@@ -522,6 +536,8 @@
             )
 
     def drain_late():
+        for g in range(OWN // GROUP):
+            drain(fwd3.at[1, pl.ds(0, 2 * GROUP)], f_recv.at[1, g])
         for kind in range(2):
             drain(send3.at[kind, pl.ds(0, PLANE - 1)], s3_send.at[kind])
             drain(fwd3.at[kind], f_send.at[kind])
@@ -529,27 +545,53 @@
     def finish_all(kind):
         pass_on(kind)
         own_heads(kind)
-        other_heads(kind)
+        if kind == 0:
+            other_heads(kind)
 
     in_order(finish_all)
     drain_late()
 
 
-def store(a, b, c, x, y, z, sem):
+def store(
+    out_q, out_k, out_v, fwd3, base_x, part_k, part_v, ks, vs, q_hbm, k_hbm, v_hbm,
+    more_k, more_v, sem,
+):
+    core = lax.axis_index("head")
+    width = OWN * DH
+    own = pl.ds(pl.multiple_of(core * width, width), width)
     part = TOK // STORE_PARTS
-    copies = []
-    for n, (src, dst) in enumerate(((a, x), (b, y), (c, z))):
-        for p in range(STORE_PARTS):
-            rows = pl.ds(p * part, part)
-            copies.append(pltpu.make_async_copy(src.at[rows], dst.at[rows], sem.at[n, p]))
-    for copy in copies:
-        copy.start()
-    for copy in copies:
-        copy.wait()
+    for p in range(STORE_PARTS):
+        rows = pl.ds(p * part, part)
+        pltpu.make_async_copy(out_k.at[rows, own], k_hbm.at[rows, own], sem.at[1]).start()
+        pltpu.make_async_copy(out_v.at[rows, own], v_hbm.at[rows, own], sem.at[2]).start()
+        pltpu.make_async_copy(out_q.at[rows], q_hbm.at[rows], sem.at[0]).start()
+    for g in range(OWN // GROUP):
+        values = []
+        for j in range(g * GROUP, (g + 1) * GROUP):
+            c = pl.ds(pl.multiple_of((1 - core) * width + j * DH, DH), DH)
+            coded = jnp.concatenate([fwd3[1, 2 * j], fwd3[1, 2 * j + 1]], axis=0)
+            hi, lo = split(decode(coded) + base_x[j])
+            vb, kb = vs[:, c], ks[:, c]
+            wide = jnp.concatenate([hi, lo], axis=1)
+            stack = jnp.concatenate([hi, lo], axis=0)
+            k_more = dot_nt(jnp.concatenate([vb, vb], axis=1), wide)
+            v_more = dot_nn(jnp.concatenate([kb, kb], axis=1), stack)
+            values.append((j, part_k[:, c] + k_more, part_v[:, c] + v_more))
+        for j, k_new, v_new in values:
+            more_k[:, j * DH : (j + 1) * DH] = k_new.astype(jnp.bfloat16)
+            more_v[:, j * DH : (j + 1) * DH] = v_new.astype(jnp.bfloat16)
+        size = GROUP * DH
+        here = pl.ds(g * size, size)
+        there = pl.ds(pl.multiple_of((1 - core) * width + g * size, size), size)
+        for p in range(2):
+            rows = pl.ds(p * BLOCK, BLOCK)
+            pltpu.make_async_copy(more_k.at[rows, here], k_hbm.at[rows, there], sem.at[1]).start()
+            pltpu.make_async_copy(more_v.at[rows, here], v_hbm.at[rows, there], sem.at[2]).start()
+    for n, ref in enumerate((out_q, out_k, out_v)):
+        pltpu.make_async_copy(ref, ref, sem.at[n]).wait()
 
 
 def body(queries, key_rows, values, out_grad, level_weights):
-    any_spec = pl.BlockSpec(memory_space=pl.ANY)
     hbm = pl.BlockSpec(memory_space=pltpu.HBM)
     vmem = pl.BlockSpec(memory_space=pltpu.VMEM)
     bf, f32 = jnp.bfloat16, jnp.float32
@@ -563,11 +605,19 @@
     grads = pl.pallas_call(
         kernel,
         name="fenwick",
-        out_shape=(pltpu.VMEM(rows, bf),) * 3,
+        out_shape=(pltpu.VMEM(rows, bf),) * 3
+        + (
+            pltpu.VMEM((2, PLANE, HALF, DH), bf),
+            pltpu.VMEM((OWN, DH, DH), f32),
+            pltpu.VMEM(rows, f32),
+            pltpu.VMEM(rows, f32),
+            pltpu.VMEM(rows, bf),
+            pltpu.VMEM(rows, bf),
+        ),
         in_specs=[hbm] * 5,
-        out_specs=(vmem,) * 3,
+        out_specs=(vmem,) * 9,
         scratch_shapes=[pltpu.SMEM((HEADS, 11), f32)]
-        + [pltpu.VMEM(rows, bf)] * 4
+        + [pltpu.VMEM(rows, bf)] * 2
         + [
             pltpu.VMEM((2, OWN, DH, DH), f32),
             pltpu.VMEM((2, OWN, DH, DH), bf),
@@ -581,10 +631,9 @@
             pltpu.VMEM((HALF, DH), f32),
             pltpu.VMEM((2, PLANE, HALF, DH), bf),
             pltpu.VMEM((2, PLANE, HALF, DH), bf),
-            pltpu.VMEM((2, PLANE, HALF, DH), bf),
             pltpu.VMEM((2, PLANE, HALF, DH), f32),
         ]
-        + [pltpu.VMEM(rows, f32)] * 3
+        + [pltpu.VMEM(rows, f32)]
         + [
             dma((5,)),
             dma((2,)),
@@ -610,9 +659,10 @@
             store,
             name="store",
             out_shape=(out, out, out),
-            in_specs=[any_spec] * 3,
+            in_specs=[vmem] * 9,
             out_specs=(hbm,) * 3,
-            scratch_shapes=[dma((3, STORE_PARTS))],
+            scratch_shapes=[pltpu.VMEM((TOK, OWN * DH), bf)] * 2 + [dma((3,))],
+            compiler_params=pltpu.CompilerParams(vmem_limit_bytes=8 << 20),
         )(*(pltpu.with_memory_space_constraint(g, pltpu.VMEM) for g in grads))
     )
 

time: 33.7 us -> 32.7 us (0.970)
  Pallas kernels: 32.9 us -> 31.9 us
    pallas_call x1, Pallas kernels: 31.2 us -> 29.9 us  [body(): pl.pallas_call(kernel, name='fenwick', out_shape=(pltpu.VMEM(rows, bf),)...]
where the time goes in v3:
time: 32.7 us; the launch traced here: 32.6 us
  Pallas kernels  31.9 us (98%)
  between operations  0.64 us (2%)
    pallas_call x1, Pallas kernels, body(): pl.pallas_call(kernel, name='fenwick', out_shape=(pltpu.VMEM(rows, bf),)...  29.9 us
    pallas_call x1, Pallas kernels, body(): pl.pallas_call(store, name='store', out_shape=(out, out, out), in_specs=[...  2.06 us

profile of v3, /device:TPU:1, one launch (start us, length us, event | category | flops | bytes accessed | tf_op | source)
XLA Modules:
  0.0 32.6 jit_solution(14784476384429346752)
XLA Ops:
  0.6 29.9 %fenwick.1 = (bf16[256,2048]{1,0:T(8,128)(2,1)S(1)}, bf16[256,2048]{1,0:T(8,128)(2,1)S(1)}, bf16[256,2048]{1,0:T(8,128)(2,1)S(1)}, bf16[2,16,64,128]{3,2,1,0:T(8...) custom-call(f32[16,11]{1,0:T(8,128)} %lw_hbm.1, ...), custom_call_target="tpu_custom_call" | custom-call | tf_op jit(solution)/shard_map/fenwick/pallas_call | solution.py:605
  30.5 2.1 %store.1 = (bf16[256,2048]{1,0:T(8,128)(2,1)}, bf16[256,2048]{1,0:T(8,128)(2,1)}, bf16[256,2048]{1,0:T(8,128)(2,1)}) custom-call(bf16[256,2048]{1,0:T(8,128)(2,1)S(1)} %get-tuple-element.12.out_q, bf16[256,2048]{1,0:T(8,128)(2,1)S(1)} %get-tuple-element.13.out_k, bf16[256,2048]{1,0:T(8,128)(2,1)S(1)} %get-tuple-element.14.out_v, ...), custom_call_target="tpu_custom_call" | custom-call | tf_op jit(solution)/shard_map/store/pallas_call | solution.py:658

commit v4 on v3

--- a/solution.py
+++ b/solution.py
@@ -11,6 +11,7 @@
 BLOCK = 128
 NX, NY, NZ = 4, 4, 8
 PLANE = NX * NY
+HEAD_ORDER = (5, 4, 3, 7, 2, 6, 1, 0)
 BACK_ORDER = sorted(
     range(PLANE), key=lambda i: (min(i % NX, NX - i % NX) + min(i // NX, NY - i // NX), i)
 )
@@ -21,7 +22,7 @@
 MESH = pl.DeviceIdType.MESH
 GROUP = 4
 LOCAL_GROUP = 2
-SPLIT_A, SPLIT_B = 10, 10
+SPLIT_A, SPLIT_B = 8, 8
 LOAD_PARTS = 2
 STORE_PARTS = 4
 PRE = float(2.0**40)
@@ -144,7 +145,7 @@
         return dot_tn(a[:, c], b[:, c])
 
     def part(j):
-        return lax.div(lax.rem(j - pair - 1 + 2 * OWN, OWN), GROUP)
+        return HEAD_ORDER.index(j) // GROUP
 
     def to_core(kind, j):
         return pltpu.make_async_remote_copy(
@@ -156,11 +157,8 @@
             device_id_type=MESH,
         )
 
-    def order(r):
-        return lax.rem(pair + 1 + r, OWN)
-
     def group(g):
-        return [order(g * GROUP + n) for n in range(GROUP)]
+        return HEAD_ORDER[g * GROUP : (g + 1) * GROUP]
 
     def states_for_sibling(kind, g):
         values = [states(kind, (1 - core) * OWN + j) for j in group(g)]

time: 32.7 us -> 32.4 us (level)
  no operation moved by 1% of the time
where the time goes in v4:
time: 32.4 us; the launch traced here: 32.3 us
  Pallas kernels  31.6 us (98%)
  between operations  0.64 us (2%)
    pallas_call x1, Pallas kernels, body(): pl.pallas_call(kernel, name='fenwick', out_shape=(pltpu.VMEM(rows, bf),)...  29.6 us
    pallas_call x1, Pallas kernels, body(): pl.pallas_call(store, name='store', out_shape=(out, out, out), in_specs=[...  2.06 us

profile of v4, /device:TPU:1, one launch (start us, length us, event | category | flops | bytes accessed | tf_op | source)
XLA Modules:
  0.0 32.3 jit_solution(7181908428000679225)
XLA Ops:
  0.6 29.6 %fenwick.1 = (bf16[256,2048]{1,0:T(8,128)(2,1)S(1)}, bf16[256,2048]{1,0:T(8,128)(2,1)S(1)}, bf16[256,2048]{1,0:T(8,128)(2,1)S(1)}, bf16[2,16,64,128]{3,2,1,0:T(8...) custom-call(f32[16,11]{1,0:T(8,128)} %lw_hbm.1, ...), custom_call_target="tpu_custom_call" | custom-call | tf_op jit(solution)/shard_map/fenwick/pallas_call | solution.py:603
  30.2 2.1 %store.1 = (bf16[256,2048]{1,0:T(8,128)(2,1)}, bf16[256,2048]{1,0:T(8,128)(2,1)}, bf16[256,2048]{1,0:T(8,128)(2,1)}) custom-call(bf16[256,2048]{1,0:T(8,128)(2,1)S(1)} %get-tuple-element.12.out_q, bf16[256,2048]{1,0:T(8,128)(2,1)S(1)} %get-tuple-element.13.out_k, bf16[256,2048]{1,0:T(8,128)(2,1)S(1)} %get-tuple-element.14.out_v, ...), custom_call_target="tpu_custom_call" | custom-call | tf_op jit(solution)/shard_map/store/pallas_call | solution.py:656

commit v5 on v4

--- a/solution.py
+++ b/solution.py
@@ -11,7 +11,7 @@
 BLOCK = 128
 NX, NY, NZ = 4, 4, 8
 PLANE = NX * NY
-HEAD_ORDER = (5, 4, 3, 7, 2, 6, 1, 0)
+HEAD_ORDER = (5, 7, 3, 4, 2, 6, 1, 0)
 BACK_ORDER = sorted(
     range(PLANE), key=lambda i: (min(i % NX, NX - i % NX) + min(i // NX, NY - i // NX), i)
 )
@@ -22,7 +22,7 @@
 MESH = pl.DeviceIdType.MESH
 GROUP = 4
 LOCAL_GROUP = 2
-SPLIT_A, SPLIT_B = 8, 8
+SPLIT_A, SPLIT_B = 6, 6
 LOAD_PARTS = 2
 STORE_PARTS = 4
 PRE = float(2.0**40)

time: 32.4 us -> 31.9 us (0.985)
  Pallas kernels: 31.6 us -> 31.1 us
    pallas_call x1, Pallas kernels: 29.6 us -> 29.1 us  [body(): pl.pallas_call(kernel, name='fenwick', out_shape=(pltpu.VMEM(rows, bf),)...]
where the time goes in v5:
time: 31.9 us; the launch traced here: 31.8 us
  Pallas kernels  31.1 us (97%)
  between operations  0.64 us (2%)
    pallas_call x1, Pallas kernels, body(): pl.pallas_call(kernel, name='fenwick', out_shape=(pltpu.VMEM(rows, bf),)...  29.1 us
    pallas_call x1, Pallas kernels, body(): pl.pallas_call(store, name='store', out_shape=(out, out, out), in_specs=[...  2.06 us

profile of v5, /device:TPU:1, one launch (start us, length us, event | category | flops | bytes accessed | tf_op | source)
XLA Modules:
  0.0 31.8 jit_solution(1529394533819284750)
XLA Ops:
  0.6 29.1 %fenwick.1 = (bf16[256,2048]{1,0:T(8,128)(2,1)S(1)}, bf16[256,2048]{1,0:T(8,128)(2,1)S(1)}, bf16[256,2048]{1,0:T(8,128)(2,1)S(1)}, bf16[2,16,64,128]{3,2,1,0:T(8...) custom-call(f32[16,11]{1,0:T(8,128)} %lw_hbm.1, ...), custom_call_target="tpu_custom_call" | custom-call | tf_op jit(solution)/shard_map/fenwick/pallas_call | solution.py:603
  29.7 2.1 %store.1 = (bf16[256,2048]{1,0:T(8,128)(2,1)}, bf16[256,2048]{1,0:T(8,128)(2,1)}, bf16[256,2048]{1,0:T(8,128)(2,1)}) custom-call(bf16[256,2048]{1,0:T(8,128)(2,1)S(1)} %get-tuple-element.12.out_q, bf16[256,2048]{1,0:T(8,128)(2,1)S(1)} %get-tuple-element.13.out_k, bf16[256,2048]{1,0:T(8,128)(2,1)S(1)} %get-tuple-element.14.out_v, ...), custom_call_target="tpu_custom_call" | custom-call | tf_op jit(solution)/shard_map/store/pallas_call | solution.py:656
